TPU v7x, 32 devices: a whole 2x2x4 slice. The times are simulated.
32 devices in a mesh: row: 4 (over y, x), col: 8 (over z, core).
Axes of the slice: x: 2, y: 2, z: 4, core: 2. Of those that a mesh axis runs over, the one named last changes fastest.
Arguments:
- feat_rows: float32 [2048, 512], P(('row', 'col')), may hold values from -0.6 to 0.6
- feat_cols: float32 [2048, 512], P(('col', 'row')), may hold values from -0.6 to 0.6
- panel_rows: float32 [2048, 1024], P(('row', 'col')), may hold values from -0.6 to 0.6
- panel_cols: float32 [2048, 1024], P(('col', 'row')), may hold values from -0.6 to 0.6
- accumulator: float32 [2048, 2048], P('row', 'col'), may hold values from -1.8 to 1.8
Outputs:
- acc_new: float32 [2048, 2048], P('row', 'col')
- grad_rows: float32 [2048, 512], P(('row', 'col'))
- grad_cols: float32 [2048, 512], P(('col', 'row'))
All inputs are finite; a program needn't handle non-finite values.
Results may differ from a plain program's by a relative error of at most 0.00011.
Values sent between devices are 32-bit elements; how exact they have to be, the bound alone decides.
A program may use at most 64 MiB of HBM per device.

v0:
```python
import functools

import jax
import jax.numpy as jnp
from jax import lax
from jax.experimental import pallas as pl
from jax.experimental.pallas import tpu as pltpu
from jax.sharding import PartitionSpec as P

decay_rate = 0.125
grad_scale = 0.25
MESH = pl.DeviceIdType.MESH
HALVES = 2
LEAD = 3
RELAY_SLOTS = 2


def split(x):
    hi = x.astype(jnp.bfloat16)
    return hi, (x - hi.astype(jnp.float32)).astype(jnp.bfloat16)


def dot3(a, b, ca, cb):
    dims = (((ca,), (cb,)), ((), ()))
    f = functools.partial(lax.dot_general, dimension_numbers=dims, preferred_element_type=jnp.float32)
    return f(a[0], b[0]) + (f(a[0], b[1]) + f(a[1], b[0]))


def order(n, depth, y, t):
    src, chunk = y * 0, t * 0
    found = y < 0
    for _ in range(depth):
        lead = t < LEAD
        done = jnp.logical_or(lead, t >= LEAD + n * y)
        take = jnp.logical_and(done, jnp.logical_not(found))
        src = jnp.where(take, y, src)
        chunk = jnp.where(take, jnp.where(lead, t, t - n * y), chunk)
        found = jnp.logical_or(found, done)
        y, t = y - 1, t - LEAD
    return src, chunk


def done_slot(n, depth, z, s):
    def seq(y):
        if y == 0:
            return [(0, i) for i in range(n)]
        own = [(y, i) for i in range(n)]
        return own[:LEAD] + seq(y - 1) + own[LEAD:]

    if s == z:
        return -1
    y, ys = (z, s) if s < z else (depth - 1 - z, depth - 1 - s)
    return max(t for t, (a, _) in enumerate(seq(y - 1)) if a == ys)


def plan(n, depth):
    table, need = [], [0] * depth
    for z in range(depth):
        shards = sorted(range(depth), key=lambda s: (done_slot(n, depth, z, s), -abs(s - z)))
        far = [s for s in shards if s != z]
        if z in (0, depth - 1):
            far.insert(len(far) - 1, z)
        else:
            far = sorted(far, key=lambda s: 2 * z + depth - 1 - s if s > z else 2 * (depth - 1 - z) + s) + [z]
        table.append(far)
        for j, s in enumerate(far):
            need[j] = max(need[j], done_slot(n, depth, z, s) + 1)
    for j in range(1, depth):
        need[j] = max(need[j], need[j - 1])
    need[0] = max(need[0], n * (depth - 2))
    for j in range(1, depth):
        need[j] = max(need[j], need[0])
    need[-1] = max(need[-1], n * (depth - 1))
    return table, need


def pick(values, at):
    out = jnp.int32(values[0])
    for i, v in enumerate(values[1:], 1):
        out = jnp.where(at == i, jnp.int32(v), out)
    return out


def kernel(R, C, fr, fc, pr, pc, acc, accv, gr_out, gc_out,
           rows, cols, chi, clo, ncol, rowp, sibp, chbuf, sumb, colacc, tacc, colr,
           lsem, rrecv, zss, sss, css, crecv, rss, rsr, chs, chrecv, gcs, gcr, ys, yr):
    me_r, me_c = lax.axis_index("row"), lax.axis_index("col")
    z, k = me_c // 2, me_c % 2
    Z = C // 2
    NR, F = fr.shape
    NC = fc.shape[0]
    Q = 1 + pr.shape[1] // F
    n = HALVES * Q
    hr = NR // HALVES
    sibling = (me_r, me_c + 1 - 2 * k)
    place = (z, Z - 1 - z)
    step_to = (2, -2)
    table, need = plan(n, Z)

    def at(start, size, mult):
        return pl.ds(pl.multiple_of(start, mult), size)

    def rchunk(c, i):
        return rows.at[i % Q, at(c * NR + (i // Q) * hr, hr, 8), :]

    def remote(src, dst, ss, rs, dev):
        return pltpu.make_async_remote_copy(src_ref=src, dst_ref=dst, send_sem=ss, recv_sem=rs, device_id=dev, device_id_type=MESH)

    def zcopy(d, zs, i):
        c = 2 * zs + k
        return remote(rchunk(c, i), rchunk(c, i), zss.at[d, zs, i], rrecv.at[c, i], (me_r, me_c + step_to[d]))

    def scopy(zs, core, i):
        c = 2 * zs + core
        return remote(rchunk(c, i), rchunk(c, i), sss.at[zs, i], rrecv.at[c, i], sibling)

    local = []
    for q in range(Q):
        rsrc = fr if q == 0 else pr.at[:, pl.ds((q - 1) * F, F)]
        csrc = fc if q == 0 else pc.at[:, pl.ds((q - 1) * F, F)]
        local.append(pltpu.make_async_copy(rsrc, rows.at[q, at(me_c * NR, NR, 8), :], lsem.at[2 * q]))
        local.append(pltpu.make_async_copy(csrc, cols.at[q, at(me_r * NC, NC, 8), :], lsem.at[2 * q + 1]))
    acc_in = pltpu.make_async_copy(acc, accv, lsem.at[2 * Q])
    for copy in local:
        copy.start()
    acc_in.start()

    barrier = pltpu.get_barrier_semaphore()

    def greet(p, carry):
        pl.semaphore_signal(barrier, inc=1, device_id=((me_r + p) % R, me_c), device_id_type=MESH)
        return carry

    lax.fori_loop(1, R, greet, 0)
    pl.semaphore_signal(barrier, inc=1, device_id=sibling, device_id_type=MESH)
    for d in range(2):
        @pl.when(place[d] < Z - 1)
        def _():
            pl.semaphore_signal(barrier, inc=1, device_id=(me_r, me_c + step_to[d]), device_id_type=MESH)
    for copy in local:
        copy.wait()
    pl.semaphore_wait(barrier, R + (z > 0).astype(jnp.int32) + (z < Z - 1).astype(jnp.int32))

    for d in range(2):
        @pl.when(place[d] < Z - 1)
        def _():
            for i in range(LEAD):
                zcopy(d, z, i).start()

    def col_send(p, q):
        block = cols.at[q, at(me_r * NC, NC, 8), :]
        return remote(block, block, css.at[p, q], crecv.at[me_r, q], ((me_r + p) % R, me_c))

    def col_recv(p, q):
        src = (me_r + p) % R
        block = cols.at[q, at(src * NC, NC, 8), :]
        return remote(block, block, css.at[p, q], crecv.at[src, q], ((me_r + p) % R, me_c))

    def push_cols(p, carry):
        for q in range(Q):
            col_send(p, q).start()
        return carry

    square = R == 4
    near = (me_r // 2 * 2 + 1 - me_r % 2, (1 - me_r // 2) * 2 + me_r % 2)
    across = R - 1 - me_r

    def own_push(axis, q):
        block = cols.at[q, at(me_r * NC, NC, 8), :]
        return remote(block, block, css.at[axis, q], crecv.at[me_r, q], (near[axis], me_c))

    def own_arrive(axis, q):
        block = cols.at[q, at(near[axis] * NC, NC, 8), :]
        return remote(block, block, css.at[axis, q], crecv.at[near[axis], q], (near[axis], me_c))

    def relay(axis, q, owner):
        block = cols.at[q, at(owner * NC + axis * (NC // 2), NC // 2, 8), :]
        return remote(block, block, ys.at[axis, q], yr.at[axis, q], (near[1 - axis], me_c))

    if square:
        for q in range(Q):
            for axis in range(2):
                own_push(axis, q).start()
    else:
        lax.fori_loop(1, R, push_cols, 0)
    for d in range(2):
        @pl.when(place[d] == 0)
        def _():
            for i in range(LEAD, n):
                zcopy(d, z, i).start()
    for i in range(n):
        scopy(z, k, i).start()

    def slot(t, carry):
        for d in range(2):
            y = place[d]

            @pl.when(t < n * y)
            def _():
                ys, i = order(n, Z, y - 1, t)
                zs = ys if d == 0 else Z - 1 - ys
                zcopy(d, zs, i).wait_recv()

                @pl.when(y < Z - 1)
                def _():
                    zcopy(d, zs, i).start()

                scopy(zs, k, i).start()

                @pl.when(jnp.logical_and(t == n * y - 1, y < Z - 1))
                def _():
                    for j in range(LEAD, n):
                        zcopy(d, z, j).start()

        return carry

    passed = 0
    if square:
        for q in range(Q):
            upto = min(RELAY_SLOTS * (q + 1), need[0])
            lax.fori_loop(passed, upto, slot, 0)
            passed = upto
            for axis in range(2):
                own_arrive(axis, q).wait_recv()
                relay(axis, q, near[axis]).start()
    lax.fori_loop(passed, need[0], slot, 0)

    def await_cols(p, carry):
        for q in range(Q):
            col_recv(p, q).wait_recv()
        return carry

    if square:
        for q in range(Q):
            for axis in range(2):
                relay(axis, q, across).wait_recv()
    else:
        lax.fori_loop(1, R, await_cols, 0)
    acc_in.wait()
    for q in range(Q):
        hi, lo = split(cols[q])
        chi[q] = hi
        clo[q] = lo
    feats = cols[0]
    ncol[...] = lax.dot_general(
        jnp.ones((8, F), jnp.float32), feats * feats, (((1,), (1,)), ((), ())),
        precision=lax.Precision.HIGHEST, preferred_element_type=jnp.float32)
    colacc[...] = jnp.zeros_like(colacc)
    tacc[...] = jnp.zeros_like(tacc)

    def shard_of(j):
        out = pick([table[0][i] for i in range(Z)], j)
        for place_z in range(1, Z):
            out = jnp.where(z == place_z, pick([table[place_z][i] for i in range(Z)], j), out)
        return out

    def exchange(zs):
        return remote(rowp.at[at(zs * 2 * NR + (1 - k) * NR, NR, 8), :], sibp.at[zs], rss.at[zs], rsr.at[zs], sibling)

    def compute(zs):
        for i in range(n):
            scopy(zs, 1 - k, i).wait_recv()
        block = at(zs * 2 * NR, 2 * NR, 8)
        f = rows[0, block, :]
        cross = lax.dot_general(f, cols[0], (((1,), (1,)), ((), ())), precision=lax.Precision.HIGHEST, preferred_element_type=jnp.float32)
        g = accv[block, :]
        for q in range(1, Q):
            g = g + dot3(split(rows[q, block, :]), (chi[q], clo[q]), 1, 1)
        accv[block, :] = g
        dist = jnp.sum(f * f, axis=1, keepdims=True) + ncol[0:1, :] - 2.0 * cross
        w = g * jnp.exp(-decay_rate * dist)
        s = jnp.sum(w, axis=1, keepdims=True)
        rowp[block, :] = grad_scale * (dot3(split(w), (chi[0], clo[0]), 1, 0) - s * f)
        exchange(zs).start()
        colacc[...] += dot3(split(w.T), split(f), 1, 0)
        tacc[...] += jnp.broadcast_to(jnp.sum(w, axis=0, keepdims=True), tacc.shape)

    def chain_copy(d, zs):
        return remote(sumb.at[zs], chbuf.at[d, zs], chs.at[zs], chrecv.at[d, zs], (me_r, me_c + step_to[d]))

    def chain(zs):
        exchange(zs).wait_recv()
        sumb[zs] = rowp[at(zs * 2 * NR + k * NR, NR, 8), :] + sibp[zs]
        for d in range(2):
            @pl.when(zs > z if d == 0 else zs < z)
            def _():
                @pl.when(place[d] > 0)
                def _():
                    chain_copy(d, zs).wait_recv()
                    sumb[zs] += chbuf[d, zs]

                chain_copy(d, zs).start()

    needs = need + [need[-1]]
    at_end = jnp.logical_or(z == 0, z == Z - 1)

    def step(j, carry):
        @pl.when(j > 0)
        def _():
            lax.fori_loop(pick(needs, j - 1), pick(needs, j), slot, 0)

        compute(shard_of(j))

        @pl.when(jnp.logical_and(at_end, j < Z - 2))
        def _():
            chain(shard_of(j))

        return carry

    lax.fori_loop(0, Z, step, 0)

    def grad_send(p):
        to = (me_r + p) % R
        return remote(colacc.at[at(to * NC, NC, 8), :], colr.at[me_r], gcs.at[p], gcr.at[me_r], (to, me_c))

    def grad_recv(p):
        src = (me_r + p) % R
        return remote(colacc.at[at(src * NC, NC, 8), :], colr.at[src], gcs.at[p], gcr.at[src], (src, me_c))

    tcol = jnp.broadcast_to(tacc[0:1, :], (128, tacc.shape[1])).T[:, 0:1]
    colacc[...] = grad_scale * (colacc[...] - tcol * cols[0])

    def push_grad(p, carry):
        grad_send(p).start()
        return carry

    lax.fori_loop(1, R, push_grad, 0)

    def last_chain(j, carry):
        chain(shard_of(j))
        return carry

    lax.fori_loop(jnp.where(at_end, max(Z - 2, 0), 0), Z, last_chain, 0)
    for d in range(2):
        @pl.when(place[d] > 0)
        def _():
            chain_copy(d, z).wait_recv()
            sumb[z] += chbuf[d, z]
    gr_out[...] = sumb[z]

    gc_out[...] = colacc[at(me_r * NC, NC, 8), :]

    def add_grad(p, carry):
        grad_recv(p).wait_recv()
        gc_out[...] += colr[(me_r + p) % R]
        return carry

    lax.fori_loop(1, R, add_grad, 0)

    def drain_peer(p, carry):
        if not square:
            for q in range(Q):
                col_send(p, q).wait_send()
        grad_send(p).wait_send()
        return carry

    lax.fori_loop(1, R, drain_peer, 0)
    if square:
        for q in range(Q):
            for axis in range(2):
                own_push(axis, q).wait_send()
                relay(axis, q, near[axis]).wait_send()
    for d in range(2):
        y = place[d]

        @pl.when(y < Z - 1)
        def _():
            def drain(ys, carry):
                zs = ys if d == 0 else Z - 1 - ys
                for i in range(n):
                    zcopy(d, zs, i).wait_send()
                return carry

            lax.fori_loop(0, y + 1, drain, 0)

    def drain_shard(zs, carry):
        for i in range(n):
            scopy(zs, k, i).wait_send()
        exchange(zs).wait_send()

        for d in range(2):
            @pl.when(zs > z if d == 0 else zs < z)
            def _():
                chain_copy(d, zs).wait_send()
        return carry

    lax.fori_loop(0, Z, drain_shard, 0)


def solution(mesh):
    R, C = mesh.shape["row"], mesh.shape["col"]
    in_specs = (
        P(("row", "col"), None),
        P(("col", "row"), None),
        P(("row", "col"), None),
        P(("col", "row"), None),
        P("row", "col"),
    )
    out_specs = (P("row", "col"), P(("row", "col"), None), P(("col", "row"), None))

    def local(fr, fc, pr, pc, acc):
        NR, F = fr.shape
        NC = fc.shape[0]
        Q = 1 + pr.shape[1] // F
        Z, n = C // 2, HALVES * Q
        f32, bf16 = jnp.float32, jnp.bfloat16
        V, D = pltpu.VMEM, pltpu.SemaphoreType.DMA
        hbm = pl.BlockSpec(memory_space=pl.ANY)
        vmem = pl.BlockSpec(memory_space=pltpu.VMEM)
        shapes = (acc.shape, fr.shape, fc.shape)
        made = pl.pallas_call(
            functools.partial(kernel, R, C),
            out_shape=tuple(pltpu.VMEM(s, f32) for s in shapes),
            in_specs=[hbm] * 5,
            out_specs=(vmem,) * 3,
            scratch_shapes=[
                V((Q, C * NR, F), f32), V((Q, R * NC, F), f32),
                V((Q, R * NC, F), bf16), V((Q, R * NC, F), bf16),
                V((8, R * NC), f32),
                V((C * NR, F), f32), V((Z, NR, F), f32), V((2, Z, NR, F), f32), V((Z, NR, F), f32),
                V((R * NC, F), f32), V((8, R * NC), f32), V((R, NC, F), f32),
                D((2 * Q + 1,)), D((C, n)), D((2, Z, n)), D((Z, n)),
                D((R, Q)), D((R, Q)), D((Z,)), D((Z,)), D((Z,)), D((2, Z)), D((R,)), D((R,)), D((2, Q)), D((2, Q)),
            ],
            compiler_params=pltpu.CompilerParams(
                collective_id=0, has_side_effects=True, vmem_limit_bytes=56 * 1024 * 1024),
        )(fr, fc, pr, pc, acc)
        return tuple(made)

    return jax.shard_map(local, mesh=mesh, in_specs=in_specs, out_specs=out_specs, check_vma=False)
```

profile of v0, /device:TPU:0, one launch (start us, length us, event | category | flops | bytes accessed | tf_op | source)
XLA Modules:
  0.0 48.7 jit_solution(2312249296472130126)
XLA Ops:
  0.6 46.0 %shard_map.76 = (f32[512,256]{1,0:T(8,128)S(1)}, f32[64,512]{1,0:T(8,128)S(1)}, f32[64,512]{1,0:T(8,128)S(1)}) custom-call(f32[64,512]{1,0:T(8,128)} %fr.1, f32[64,512]{1,0:T(8,128)} %fc.1, f32[64,1024]{1,0:T(8,128)} %pr.1, f32[64,1024]{1,0:T(8,128)} %pc.1, f32[512,256]{1,0:T(8,128)} %acc.1), custom_call_target="tpu_custom_call" | custom-call | tf_op jit(solution)/shard_map/pallas_call | solution.py:411
  46.6 0.8 %copy.11 = f32[512,256]{1,0:T(8,128)} copy(f32[512,256]{1,0:T(8,128)S(1)} %get-tuple-element.3) | data formatting | bytes 1048576
  47.4 0.7 %copy.12 = f32[64,512]{1,0:T(8,128)} copy(f32[64,512]{1,0:T(8,128)S(1)} %get-tuple-element.4) | data formatting | bytes 262144
  48.1 0.7 %copy.13 = f32[64,512]{1,0:T(8,128)} copy(f32[64,512]{1,0:T(8,128)S(1)} %get-tuple-element.5) | data formatting | bytes 262144
where the time goes:
time: 48.9 us; the launch traced here: 48.7 us
  Pallas kernels  46 us (94%)
  local copies, waits for them, and re-layouts  2.11 us (4%)
  between operations  0.64 us (1%)
    pallas_call x1, Pallas kernels, local(): pl.pallas_call(functools.partial(kernel, R, C), out_shape=tuple((pltpu.VM...  46 us
    unnamed x3, local copies, waits for them, and re-layouts  2.11 us

commit v1 on v0

v1 whole, which is shorter than its diff:
```python
import functools

import jax
import jax.numpy as jnp
from jax import lax
from jax.experimental import pallas as pl
from jax.experimental.pallas import tpu as pltpu
from jax.sharding import PartitionSpec as P

decay_rate = 0.125
grad_scale = 0.25
MESH = pl.DeviceIdType.MESH
HALVES = 2
LEAD = 4
RELAY_SLOTS = 2
LATE = 2


def split(x):
    hi = x.astype(jnp.bfloat16)
    return hi, (x - hi.astype(jnp.float32)).astype(jnp.bfloat16)


def dot3(a, b, ca, cb):
    dims = (((ca,), (cb,)), ((), ()))
    f = functools.partial(lax.dot_general, dimension_numbers=dims, preferred_element_type=jnp.float32)
    return f(a[0], b[0]) + (f(a[0], b[1]) + f(a[1], b[0]))


def order(n, depth, y, t):
    src, chunk = y * 0, t * 0
    found = y < 0
    for _ in range(depth):
        lead = t < LEAD
        done = jnp.logical_or(lead, t >= LEAD + n * y)
        take = jnp.logical_and(done, jnp.logical_not(found))
        src = jnp.where(take, y, src)
        chunk = jnp.where(take, jnp.where(lead, t, t - n * y), chunk)
        found = jnp.logical_or(found, done)
        y, t = y - 1, t - LEAD
    return src, chunk


def ready(n, depth, z, s, chunks):
    def seq(y):
        own = [(y, i) for i in range(n)]
        return own if y == 0 else own[:LEAD] + seq(y - 1) + own[LEAD:]

    if s == z:
        return 0
    y, ys = (z, s) if s < z else (depth - 1 - z, depth - 1 - s)
    return 1 + max(t for t, (a, i) in enumerate(seq(y - 1)) if a == ys and i in chunks)


def plan(Q, depth):
    n = HALVES * Q
    table, need = [], []
    steps = [(2 * j, 2 * j + 1) for j in range(HALVES * depth // 2 - 1)]
    steps += [(HALVES * depth - 2,), (HALVES * depth - 1,)]
    for z in range(depth):
        own = [(z, h) for h in range(HALVES)]
        far = [(s, h) for s in range(depth) for h in range(HALVES) if s != z]
        at = {(s, h): ready(n, depth, z, s, range(h * Q, h * Q + Q)) for s, h in own + far}
        far = sorted(far, key=lambda u: (at[u], -abs(u[0] - z)))
        end = z in (0, depth - 1)
        subs = own + far if end else far + own
        total = n * max(z, depth - 1 - z)
        late = max(ready(n, depth, z, s, (h * Q,)) for s, h in subs[-LATE:])
        first = min(total, max(late, n + LEAD - 1)) if end else total
        taken, row = first, []
        for j, step in enumerate(steps):
            taken = max(taken, min(total, max(at[subs[i]] for i in step) + 1) if j else first)
            row.append(taken)
        table.append([s * HALVES + h for s, h in subs])
        need.append(row)
    return table, need


def pick(values, at):
    out = jnp.int32(values[0])
    for i, v in enumerate(values[1:], 1):
        out = jnp.where(at == i, jnp.int32(v), out)
    return out


def kernel(R, C, fr, fc, pr, pc, acc, accv, gr_out, gc_out,
           rows, cols, chi, clo, ncol, rowp, sibp, sumb, rgbuf, colacc, tacc, colr, lfeat, wlate, wlin,
           lsem, rrecv, srecv, crecv, xrecv, sends, bulk):
    me_r, me_c = lax.axis_index("row"), lax.axis_index("col")
    z, k = me_c // 2, me_c % 2
    Z = C // 2
    NR, F = fr.shape
    NC = fc.shape[0]
    Q = 1 + pr.shape[1] // F
    n = HALVES * Q
    hr = NR // HALVES
    UR = 2 * hr
    sibling = (me_r, me_c + 1 - 2 * k)
    place = (z, Z - 1 - z)
    step_to = (2, -2)
    table, need = plan(Q, Z)
    square = R == 4
    near = (me_r // 2 * 2 + 1 - me_r % 2, (1 - me_r // 2) * 2 + me_r % 2)
    across = R - 1 - me_r
    z_sent, sib_sent, col_sent, relay_sent, x_sent, row_sent, grad_sent, w_sent, feat_sent, pass_sent = (
        sends.at[i] for i in (0, 2, 3, 4, 5, 6, 7, 8, 9, 10))
    relay_in, row_in, grad_in, w_in, feat_in, pass_in = (bulk.at[i] for i in range(6))

    def at(start, size, mult):
        return pl.ds(pl.multiple_of(start, mult), size)

    def remote(src, dst, ss, rs, dev):
        return pltpu.make_async_remote_copy(src_ref=src, dst_ref=dst, send_sem=ss, recv_sem=rs, device_id=dev, device_id_type=MESH)

    def landed(ref, sem):
        pltpu.make_async_copy(ref, ref, sem).wait()

    def place_of(zs, h, core):
        return ((zs * HALVES + h) * 2 + core) * hr

    def rchunk(zs, core, i):
        return rows.at[i % Q, at(place_of(zs, i // Q, core), hr, 8), :]

    def own_chunk(i):
        q, h = i % Q, i // Q
        src = fr if q == 0 else pr
        return src.at[pl.ds(h * hr, hr), pl.ds(max(q - 1, 0) * F, F)]

    def own_cols(q):
        return fc if q == 0 else pc.at[:, pl.ds((q - 1) * F, F)]

    def zcopy(d, zs, i, src=None):
        dst = rchunk(zs, k, i)
        return remote(dst if src is None else src, dst, sends.at[d], rrecv.at[zs, i], (me_r, me_c + step_to[d]))

    def scopy(zs, i, src=None):
        dst = rchunk(zs, k, i)
        return remote(dst if src is None else src, dst, sib_sent, srecv.at[zs * HALVES + i // Q], sibling)

    for q in range(Q):
        for h in range(HALVES):
            pltpu.make_async_copy(own_chunk(h * Q + q), rchunk(z, k, h * Q + q), lsem.at[0]).start()
        pltpu.make_async_copy(own_cols(q), cols.at[q, at(me_r * NC, NC, 8), :], lsem.at[1]).start()
    acc_in = pltpu.make_async_copy(acc, accv, lsem.at[2])
    acc_in.start()

    barrier = pltpu.get_barrier_semaphore()
    if square:
        for axis in range(2):
            pl.semaphore_signal(barrier, inc=1, device_id=(near[axis], me_c), device_id_type=MESH)
    else:
        def greet(p, carry):
            pl.semaphore_signal(barrier, inc=1, device_id=((me_r + p) % R, me_c), device_id_type=MESH)
            return carry

        lax.fori_loop(1, R, greet, 0)
    pl.semaphore_signal(barrier, inc=1, device_id=sibling, device_id_type=MESH)
    for d in range(2):
        @pl.when(place[d] < Z - 1)
        def _():
            pl.semaphore_signal(barrier, inc=1, device_id=(me_r, me_c + step_to[d]), device_id_type=MESH)
    greeted = (2 if square else R - 1) + 1
    pl.semaphore_wait(barrier, greeted + (z > 0).astype(jnp.int32) + (z < Z - 1).astype(jnp.int32))

    def zown(d, lo, hi):
        for i in range(lo, hi):
            zcopy(d, z, i, own_chunk(i)).start()

    for d in range(2):
        @pl.when(place[d] < Z - 1)
        def _():
            zown(d, 0, LEAD)

    def own_push(axis, q):
        block = cols.at[q, at(me_r * NC, NC, 8), :]
        return remote(own_cols(q), block, col_sent, crecv.at[axis, q], (near[axis], me_c))

    def own_arrive(axis, q):
        block = cols.at[q, at(near[axis] * NC, NC, 8), :]
        return remote(block, block, col_sent, crecv.at[axis, q], (near[axis], me_c))

    def relay(axis, q):
        block = cols.at[q, at(near[axis] * NC + axis * (NC // 2), NC // 2, 8), :]
        return remote(block, block, relay_sent, relay_in, (near[1 - axis], me_c))

    def push_cols(p, carry):
        for q in range(Q):
            block = cols.at[q, at(me_r * NC, NC, 8), :]
            remote(own_cols(q), block, col_sent, relay_in, ((me_r + p) % R, me_c)).start()
        return carry

    if square:
        for q in range(Q):
            for axis in range(2):
                own_push(axis, q).start()
    else:
        lax.fori_loop(1, R, push_cols, 0)
    for d in range(2):
        @pl.when(place[d] == 0)
        def _():
            zown(d, LEAD, n)
    for i in range(n):
        scopy(z, i, own_chunk(i)).start()

    def slot(t, carry):
        for d in range(2):
            y = place[d]

            @pl.when(t < n * y)
            def _():
                ys, i = order(n, Z, y - 1, t)
                zs = ys if d == 0 else Z - 1 - ys
                zcopy(d, zs, i).wait_recv()

                @pl.when(y < Z - 1)
                def _():
                    zcopy(d, zs, i).start()

                scopy(zs, i).start()

                @pl.when(jnp.logical_and(t == n * y - 1, y < Z - 1))
                def _():
                    zown(d, LEAD, n)

        return carry

    def by_place(values, j):
        out = pick([row[j] for row in values], z) if isinstance(j, int) else None
        if out is None:
            out = pick(values[0], j)
            for place_z in range(1, Z):
                out = jnp.where(z == place_z, pick(values[place_z], j), out)
        return out

    first = by_place(need, 0)
    passed = 0
    if square:
        for q in range(Q):
            upto = min(RELAY_SLOTS * (q + 1), min(row[0] for row in need))
            lax.fori_loop(passed, upto, slot, 0)
            passed = upto
            for axis in range(2):
                own_arrive(axis, q).wait_recv()
                relay(axis, q).start()
    lax.fori_loop(passed, first, slot, 0)

    landed(rows.at[:, pl.ds(0, NR), :], lsem.at[0])
    landed(cols.at[:, pl.ds(0, NC), :], lsem.at[1])
    acc_in.wait()
    landed(cols.at[:, pl.ds(0, NC if square else (R - 1) * NC), :], relay_in)

    late = [by_place(table, HALVES * Z - LATE + s) for s in range(LATE)]

    def push_late(p, carry):
        for s in range(LATE):
            src = rows.at[0, at(late[s] * UR + k * hr, hr, 8), :]
            remote(src, lfeat.at[me_r, s, k], feat_sent, feat_in, ((me_r + p) % R, me_c)).start()
        return carry

    lax.fori_loop(1, R, push_late, 0)

    for q in range(Q):
        hi, lo = split(cols[q])
        chi[q] = hi
        clo[q] = lo
    feats = cols[0]
    ncol[...] = lax.dot_general(
        jnp.ones((8, F), jnp.float32), feats * feats, (((1,), (1,)), ((), ())),
        precision=lax.Precision.HIGHEST, preferred_element_type=jnp.float32)
    colacc[...] = jnp.zeros_like(colacc)
    tacc[...] = jnp.zeros_like(tacc)

    def exchange(sub):
        return remote(rowp.at[at(sub * UR + (1 - k) * hr, hr, 8), :], sibp.at[sub], x_sent, xrecv.at[sub], sibling)

    def weigh(subs):
        for sub in subs:
            landed(rows.at[:, pl.ds(0, hr), :], srecv.at[sub])
        blocks = [at(sub * UR, UR, 8) for sub in subs]
        parts = [at((2 * (sub // HALVES) + core) * NR + sub % HALVES * hr, hr, 8) for sub in subs for core in range(2)]
        f = jnp.concatenate([rows[0, b, :] for b in blocks], axis=0)
        cross = lax.dot_general(f, cols[0], (((1,), (1,)), ((), ())), precision=lax.Precision.HIGHEST, preferred_element_type=jnp.float32)
        g = jnp.concatenate([accv[b, :] for b in parts], axis=0)
        for q in range(1, Q):
            panel = jnp.concatenate([rows[q, b, :] for b in blocks], axis=0)
            g = g + dot3(split(panel), (chi[q], clo[q]), 1, 1)
        for i, b in enumerate(parts):
            accv[b, :] = g[i * hr:(i + 1) * hr, :]
        dist = jnp.sum(f * f, axis=1, keepdims=True) + ncol[0:1, :] - 2.0 * cross
        return f, g * jnp.exp(-decay_rate * dist)

    def row_part(subs, f, w):
        s = jnp.sum(w, axis=1, keepdims=True)
        part = grad_scale * (dot3(split(w), (chi[0], clo[0]), 1, 0) - s * f)
        for i, sub in enumerate(subs):
            rowp[at(sub * UR, UR, 8), :] = part[i * UR:(i + 1) * UR, :]
        for sub in subs:
            exchange(sub).start()

    def finish(subs):
        for sub in subs:
            exchange(sub).wait_recv()
            zs, h = sub // HALVES, sub % HALVES
            total = rowp[at(sub * UR + k * hr, hr, 8), :] + sibp[sub]

            @pl.when(zs == z)
            def _():
                rgbuf[z, at(h * hr, hr, 8), :] = total

            @pl.when(zs != z)
            def _():
                sumb[sub] = total
                remote(sumb.at[sub], rgbuf.at[z, at(h * hr, hr, 8), :], row_sent, row_in, (me_r, 2 * zs + k)).start()

    pairs = HALVES * Z // 2 - 1

    def pair_at(j):
        return [by_place(table, 2 * j + i) for i in range(2)]

    def step(j, carry):
        @pl.when(j > 0)
        def _():
            lax.fori_loop(by_place(need, j - 1), by_place(need, j), slot, 0)
            finish(pair_at(j - 1))

        subs = pair_at(j)
        f, w = weigh(subs)
        row_part(subs, f, w)
        colacc[...] += dot3(split(w.T), split(f), 1, 0)
        tacc[...] += jnp.broadcast_to(jnp.sum(w, axis=0, keepdims=True), tacc.shape)
        return carry

    lax.fori_loop(0, pairs, step, 0)

    tcol = jnp.broadcast_to(tacc[0:1, :], (128, tacc.shape[1])).T[:, 0:1]
    colacc[...] = grad_scale * (colacc[...] - tcol * cols[0])

    def push_grad(p, carry):
        to = (me_r + p) % R
        remote(colacc.at[at(to * NC, NC, 8), :], colr.at[me_r], grad_sent, grad_in, (to, me_c)).start()
        return carry

    lax.fori_loop(1, R, push_grad, 0)
    finish(pair_at(jnp.int32(pairs - 1)))

    landed(lfeat.at[pl.ds(0, R - 1), :, 0], feat_in)

    def pass_on(p, carry):
        block = lfeat.at[(me_r + p) % R, :, k]
        remote(block, block, pass_sent, pass_in, sibling).start()
        return carry

    lax.fori_loop(1, R, pass_on, 0)

    for s in range(LATE):
        lax.fori_loop(by_place(need, pairs + s - 1), by_place(need, pairs + s), slot, 0)
        if s:
            finish([late[s - 1]])
        f, w = weigh([late[s]])
        wlate[:, s * UR:(s + 1) * UR] = w.T
        for core in range(2):
            lfeat[me_r, s, core] = f[core * hr:(core + 1) * hr, :]
        if s == LATE - 1:
            def push_w(p, carry):
                to = (me_r + p) % R
                remote(wlate.at[at(to * NC, NC, 8), :], wlin.at[me_r], w_sent, w_in, (to, me_c)).start()
                return carry

            lax.fori_loop(1, R, push_w, 0)
            wlin[me_r] = wlate[at(me_r * NC, NC, 8), :]
        row_part([late[s]], f, w)

    landed(lfeat.at[pl.ds(0, R - 1), :, 0], pass_in)
    behind = split(lfeat[...].reshape(R * LATE * UR, F))
    finish([late[LATE - 1]])
    landed(colr.at[pl.ds(0, R - 1)], grad_in)
    mine = at(me_r * NC, NC, 8)
    gc_out[...] = colacc[mine, :]

    def add_grad(p, carry):
        gc_out[...] += colr[(me_r + p) % R]
        return carry

    lax.fori_loop(1, R, add_grad, 0)
    landed(wlin.at[pl.ds(0, R - 1)], w_in)
    w = jnp.concatenate([wlin[p] for p in range(R)], axis=1)
    gc_out[...] += grad_scale * (dot3(split(w), behind, 1, 0) - jnp.sum(w, axis=1, keepdims=True) * cols[0, mine, :])

    landed(rgbuf.at[pl.ds(0, Z - 1)], row_in)
    total = rgbuf[0]
    for zs in range(1, Z):
        total = total + rgbuf[zs]
    gr_out[...] = total

    for d in range(2):
        for y in range(Z - 1):
            @pl.when(place[d] == y)
            def _():
                landed(rows.at[:, pl.ds(0, (y + 1) * NR), :], sends.at[d])
    landed(rows.at[:, pl.ds(0, Z * NR), :], sib_sent)
    landed(cols.at[:, pl.ds(0, (2 if square else R - 1) * NC), :], col_sent)
    if square:
        landed(cols.at[:, pl.ds(0, NC), :], relay_sent)
    landed(sibp, x_sent)
    landed(rgbuf.at[pl.ds(0, Z - 1)], row_sent)
    landed(colr.at[pl.ds(0, R - 1)], grad_sent)
    landed(wlin.at[pl.ds(0, R - 1)], w_sent)
    landed(lfeat.at[pl.ds(0, R - 1), :, 0], feat_sent)
    landed(lfeat.at[pl.ds(0, R - 1), :, 0], pass_sent)


def put(a, b, c, x, y, w, sem):
    copies = [pltpu.make_async_copy(u, v, sem.at[i]) for i, (u, v) in enumerate(((a, x), (b, y), (c, w)))]
    for copy in copies:
        copy.start()
    for copy in copies:
        copy.wait()


def solution(mesh):
    R, C = mesh.shape["row"], mesh.shape["col"]
    in_specs = (
        P(("row", "col"), None),
        P(("col", "row"), None),
        P(("row", "col"), None),
        P(("col", "row"), None),
        P("row", "col"),
    )
    out_specs = (P("row", "col"), P(("row", "col"), None), P(("col", "row"), None))

    def local(fr, fc, pr, pc, acc):
        NR, F = fr.shape
        NC = fc.shape[0]
        Q = 1 + pr.shape[1] // F
        Z, n = C // 2, HALVES * Q
        hr, subs = NR // HALVES, HALVES * (C // 2)
        f32, bf16 = jnp.float32, jnp.bfloat16
        V, D = pltpu.VMEM, pltpu.SemaphoreType.DMA
        hbm = pl.BlockSpec(memory_space=pl.ANY)
        vmem = pl.BlockSpec(memory_space=pltpu.VMEM)
        shapes = (acc.shape, fr.shape, fc.shape)
        made = pl.pallas_call(
            functools.partial(kernel, R, C),
            out_shape=tuple(pltpu.VMEM(s, f32) for s in shapes),
            in_specs=[hbm] * 5,
            out_specs=(vmem,) * 3,
            scratch_shapes=[
                V((Q, C * NR, F), f32), V((Q, R * NC, F), f32),
                V((Q, R * NC, F), bf16), V((Q, R * NC, F), bf16),
                V((8, R * NC), f32),
                V((C * NR, F), f32), V((subs, hr, F), f32), V((subs, hr, F), f32), V((Z, NR, F), f32),
                V((R * NC, F), f32), V((8, R * NC), f32), V((R, NC, F), f32),
                V((R, LATE, 2, hr, F), f32), V((R * NC, LATE * 2 * hr), f32), V((R, NC, LATE * 2 * hr), f32),
                D((3,)), D((Z, n)), D((subs,)), D((2, Q)), D((subs,)), D((11,)), D((6,)),
            ],
            compiler_params=pltpu.CompilerParams(
                collective_id=0, has_side_effects=True, vmem_limit_bytes=56 * 1024 * 1024),
        )(fr, fc, pr, pc, acc)
        made = [pltpu.with_memory_space_constraint(m, pltpu.VMEM) for m in made]
        done = pl.pallas_call(
            put,
            out_shape=tuple(jax.ShapeDtypeStruct(s, f32) for s in shapes),
            in_specs=[vmem] * 3,
            out_specs=(hbm,) * 3,
            scratch_shapes=[D((3,))],
        )(*made)
        return tuple(done)

    return jax.shard_map(local, mesh=mesh, in_specs=in_specs, out_specs=out_specs, check_vma=False)
```

time: 48.9 us -> 45.8 us (0.937)
  local copies, waits for them, and re-layouts: 2.11 us -> 0 us
  Pallas kernels: 46 us -> 44.9 us
    unnamed x3 -> x0, local copies, waits for them, and re-layouts: 2.11 us -> none
    pallas_call x1, Pallas kernels: 46 us -> 44 us  [local(): pl.pallas_call(functools.partial(kernel, R, C), out_shape=tuple((pltpu.VM...]
    pallas_call x0 -> x1, Pallas kernels: none -> 0.9 us  [local(): pl.pallas_call(put, out_shape=tuple((jax.ShapeDtypeStruct(s, f32) for s i...]
where the time goes in v1:
time: 45.8 us; the launch traced here: 45.6 us
  Pallas kernels  44.9 us (98%)
  between operations  0.64 us (1%)
    pallas_call x1, Pallas kernels, local(): pl.pallas_call(functools.partial(kernel, R, C), out_shape=tuple((pltpu.VM...  44 us

profile of v1, /device:TPU:0, one launch (start us, length us, event | category | flops | bytes accessed | tf_op | source)
XLA Modules:
  0.0 45.6 jit_solution(13122990101910723606)
XLA Ops:
  0.6 44.0 %shard_map.76 = (f32[512,256]{1,0:T(8,128)S(1)}, f32[64,512]{1,0:T(8,128)S(1)}, f32[64,512]{1,0:T(8,128)S(1)}) custom-call(f32[64,512]{1,0:T(8,128)} %fr.1, f32[64,512]{1,0:T(8,128)} %fc.1, f32[64,1024]{1,0:T(8,128)} %pr.1, f32[64,1024]{1,0:T(8,128)} %pc.1, f32[512,256]{1,0:T(8,128)} %acc.1), custom_call_target="tpu_custom_call" | custom-call | tf_op jit(solution)/shard_map/pallas_call | solution.py:442
  44.7 0.9 %shard_map.77 = (f32[512,256]{1,0:T(8,128)}, f32[64,512]{1,0:T(8,128)}, f32[64,512]{1,0:T(8,128)}) custom-call(f32[512,256]{1,0:T(8,128)S(1)} %get-tuple-element.6.a, f32[64,512]{1,0:T(8,128)S(1)} %get-tuple-element.7.b, f32[64,512]{1,0:T(8,128)S(1)} %get-tuple-element.8.c), custom_call_target="tpu_custom_call" | custom-call | tf_op jit(solution)/shard_map/pallas_call | solution.py:460

commit v2 on v1

--- a/solution.py
+++ b/solution.py
@@ -25,6 +25,20 @@
     dims = (((ca,), (cb,)), ((), ()))
     f = functools.partial(lax.dot_general, dimension_numbers=dims, preferred_element_type=jnp.float32)
     return f(a[0], b[0]) + (f(a[0], b[1]) + f(a[1], b[0]))
+
+
+def split3(x):
+    hi = x.astype(jnp.bfloat16)
+    rest = x - hi.astype(jnp.float32)
+    mid = rest.astype(jnp.bfloat16)
+    return hi, mid, (rest - mid.astype(jnp.float32)).astype(jnp.bfloat16)
+
+
+def dot6(a, b, ca, cb):
+    dims = (((ca,), (cb,)), ((), ()))
+    f = functools.partial(lax.dot_general, dimension_numbers=dims, preferred_element_type=jnp.float32)
+    low = f(a[0], b[2]) + (f(a[2], b[0]) + f(a[1], b[1]))
+    return f(a[0], b[0]) + ((f(a[0], b[1]) + f(a[1], b[0])) + low)
 
 
 def order(n, depth, y, t):
@@ -54,7 +68,7 @@
 
 def plan(Q, depth):
     n = HALVES * Q
-    table, need = [], []
+    table, need, early = [], [], []
     steps = [(2 * j, 2 * j + 1) for j in range(HALVES * depth // 2 - 1)]
     steps += [(HALVES * depth - 2,), (HALVES * depth - 1,)]
     for z in range(depth):
@@ -66,14 +80,15 @@
         subs = own + far if end else far + own
         total = n * max(z, depth - 1 - z)
         late = max(ready(n, depth, z, s, (h * Q,)) for s, h in subs[-LATE:])
-        first = min(total, max(late, n + LEAD - 1)) if end else total
-        taken, row = first, []
+        first = min(total, max(late, n + LEAD - 1))
+        early.append((first, first if end else max(first, total - 1)))
+        taken, row = first if end else total, []
         for j, step in enumerate(steps):
-            taken = max(taken, min(total, max(at[subs[i]] for i in step) + 1) if j else first)
+            taken = max(taken, min(total, max(at[subs[i]] for i in step) + 1) if j else taken)
             row.append(taken)
         table.append([s * HALVES + h for s, h in subs])
         need.append(row)
-    return table, need
+    return table, need, early
 
 
 def pick(values, at):
@@ -84,7 +99,7 @@
 
 
 def kernel(R, C, fr, fc, pr, pc, acc, accv, gr_out, gc_out,
-           rows, cols, chi, clo, ncol, rowp, sibp, sumb, rgbuf, colacc, tacc, colr, lfeat, wlate, wlin,
+           rows, cols, chi, clo, cend, ncol, rowp, sibp, sumb, inbox, csum, colacc, tacc, colr, lfeat, lkern, wlate, wlin,
            lsem, rrecv, srecv, crecv, xrecv, sends, bulk):
     me_r, me_c = lax.axis_index("row"), lax.axis_index("col")
     z, k = me_c // 2, me_c % 2
@@ -98,13 +113,13 @@
     sibling = (me_r, me_c + 1 - 2 * k)
     place = (z, Z - 1 - z)
     step_to = (2, -2)
-    table, need = plan(Q, Z)
+    table, need, early = plan(Q, Z)
     square = R == 4
     near = (me_r // 2 * 2 + 1 - me_r % 2, (1 - me_r // 2) * 2 + me_r % 2)
     across = R - 1 - me_r
     z_sent, sib_sent, col_sent, relay_sent, x_sent, row_sent, grad_sent, w_sent, feat_sent, pass_sent = (
         sends.at[i] for i in (0, 2, 3, 4, 5, 6, 7, 8, 9, 10))
-    relay_in, row_in, grad_in, w_in, feat_in, pass_in = (bulk.at[i] for i in range(6))
+    grad_in, w_in, feat_in, pass_in, relay_in = (bulk.at[i] for i in range(2, 7))
 
     def at(start, size, mult):
         return pl.ds(pl.multiple_of(start, mult), size)
@@ -135,7 +150,7 @@
 
     def scopy(zs, i, src=None):
         dst = rchunk(zs, k, i)
-        return remote(dst if src is None else src, dst, sib_sent, srecv.at[zs * HALVES + i // Q], sibling)
+        return remote(dst if src is None else src, dst, sib_sent, srecv.at[zs * HALVES + i // Q, min(i % Q, 1) if isinstance(i, int) else (i % Q > 0).astype(jnp.int32)], sibling)
 
     for q in range(Q):
         for h in range(HALVES):
@@ -232,17 +247,16 @@
                 out = jnp.where(z == place_z, pick(values[place_z], j), out)
         return out
 
-    first = by_place(need, 0)
     passed = 0
     if square:
         for q in range(Q):
-            upto = min(RELAY_SLOTS * (q + 1), min(row[0] for row in need))
+            upto = min(RELAY_SLOTS * (q + 1), min(row[0] for row in early))
             lax.fori_loop(passed, upto, slot, 0)
             passed = upto
             for axis in range(2):
                 own_arrive(axis, q).wait_recv()
                 relay(axis, q).start()
-    lax.fori_loop(passed, first, slot, 0)
+    lax.fori_loop(passed, by_place(early, 0), slot, 0)
 
     landed(rows.at[:, pl.ds(0, NR), :], lsem.at[0])
     landed(cols.at[:, pl.ds(0, NC), :], lsem.at[1])
@@ -264,30 +278,38 @@
         chi[q] = hi
         clo[q] = lo
     feats = cols[0]
-    ncol[...] = lax.dot_general(
-        jnp.ones((8, F), jnp.float32), feats * feats, (((1,), (1,)), ((), ())),
-        precision=lax.Precision.HIGHEST, preferred_element_type=jnp.float32)
+    cend[...] = split3(feats)[2]
+    ones = jnp.ones((8, F), jnp.bfloat16)
+    ncol[...] = sum(lax.dot_general(
+        ones, piece, (((1,), (1,)), ((), ())), preferred_element_type=jnp.float32) for piece in reversed(split3(feats * feats)))
     colacc[...] = jnp.zeros_like(colacc)
     tacc[...] = jnp.zeros_like(tacc)
 
     def exchange(sub):
         return remote(rowp.at[at(sub * UR + (1 - k) * hr, hr, 8), :], sibp.at[sub], x_sent, xrecv.at[sub], sibling)
 
-    def weigh(subs):
+    def take(subs, q):
         for sub in subs:
-            landed(rows.at[:, pl.ds(0, hr), :], srecv.at[sub])
-        blocks = [at(sub * UR, UR, 8) for sub in subs]
+            landed(rows.at[:Q - 1 if q else 1, pl.ds(0, hr), :], srecv.at[sub, min(q, 1)])
+
+    def kern(subs):
+        take(subs, 0)
+        f = jnp.concatenate([rows[0, at(sub * UR, UR, 8), :] for sub in subs], axis=0)
+        pieces = split3(f)
+        cross = dot6(pieces, (chi[0], clo[0], cend[...]), 1, 1)
+        dist = jnp.sum(f * f, axis=1, keepdims=True) + ncol[0:1, :] - 2.0 * cross
+        return f, pieces, jnp.exp(-decay_rate * dist)
+
+    def gram(subs):
+        take(subs, 1)
         parts = [at((2 * (sub // HALVES) + core) * NR + sub % HALVES * hr, hr, 8) for sub in subs for core in range(2)]
-        f = jnp.concatenate([rows[0, b, :] for b in blocks], axis=0)
-        cross = lax.dot_general(f, cols[0], (((1,), (1,)), ((), ())), precision=lax.Precision.HIGHEST, preferred_element_type=jnp.float32)
         g = jnp.concatenate([accv[b, :] for b in parts], axis=0)
         for q in range(1, Q):
-            panel = jnp.concatenate([rows[q, b, :] for b in blocks], axis=0)
+            panel = jnp.concatenate([rows[q, at(sub * UR, UR, 8), :] for sub in subs], axis=0)
             g = g + dot3(split(panel), (chi[q], clo[q]), 1, 1)
         for i, b in enumerate(parts):
             accv[b, :] = g[i * hr:(i + 1) * hr, :]
-        dist = jnp.sum(f * f, axis=1, keepdims=True) + ncol[0:1, :] - 2.0 * cross
-        return f, g * jnp.exp(-decay_rate * dist)
+        return g
 
     def row_part(subs, f, w):
         s = jnp.sum(w, axis=1, keepdims=True)
@@ -297,37 +319,67 @@
         for sub in subs:
             exchange(sub).start()
 
+    def inward(end):
+        return 1 if end == 0 else Z - 2
+
     def finish(subs):
         for sub in subs:
             exchange(sub).wait_recv()
             zs, h = sub // HALVES, sub % HALVES
             total = rowp[at(sub * UR + k * hr, hr, 8), :] + sibp[sub]
-
-            @pl.when(zs == z)
+            own = zs == z
+            group = jnp.where(own, 0, jnp.where(zs == 0, 1, jnp.where(zs == Z - 1, 2, 0)))
+            to = jnp.where(group == 0, zs, jnp.where(group == 1, inward(0), inward(1)))
+            dst = inbox.at[group * Z + z, at(h * hr, hr, 8), :]
+
+            @pl.when(to == z)
             def _():
-                rgbuf[z, at(h * hr, hr, 8), :] = total
-
-            @pl.when(zs != z)
+                dst[...] = total
+
+            @pl.when(to != z)
             def _():
                 sumb[sub] = total
-                remote(sumb.at[sub], rgbuf.at[z, at(h * hr, hr, 8), :], row_sent, row_in, (me_r, 2 * zs + k)).start()
+                remote(sumb.at[sub], dst, row_sent, bulk.at[jnp.minimum(group, 1)], (me_r, 2 * to + k)).start()
+
+    def collect():
+        for e, end in enumerate((0, Z - 1)):
+            @pl.when(jnp.logical_and(z == inward(end), z != end))
+            def _():
+                if Z > 2:
+                    landed(inbox.at[pl.ds(0, Z - 2)], bulk.at[1])
+                terms = [inbox[(e + 1) * Z + zs] for zs in range(Z) if zs != end]
+                csum[e] = sum(terms[1:], terms[0])
+                remote(csum.at[e], inbox.at[z], row_sent, bulk.at[0], (me_r, 2 * end + k)).start()
 
     pairs = HALVES * Z // 2 - 1
 
     def pair_at(j):
         return [by_place(table, 2 * j + i) for i in range(2)]
+
+    lax.fori_loop(by_place(early, 0), by_place(early, 1), slot, 0)
+    f, _, weight = kern(late)
+    lkern[...] = weight
+    for s in range(LATE):
+        for core in range(2):
+            lfeat[me_r, s, core] = f[(2 * s + core) * hr:(2 * s + core + 1) * hr, :]
+    lax.fori_loop(by_place(early, 1), by_place(need, 0), slot, 0)
 
     def step(j, carry):
         @pl.when(j > 0)
         def _():
             lax.fori_loop(by_place(need, j - 1), by_place(need, j), slot, 0)
+
+        subs = pair_at(j)
+        f, pieces, weight = kern(subs)
+        w = gram(subs) * weight
+        row_part(subs, f, w)
+        colacc[...] += dot3(split(w.T), pieces[:2], 1, 0)
+        tacc[...] += jnp.broadcast_to(jnp.sum(w, axis=0, keepdims=True), tacc.shape)
+
+        @pl.when(j > 0)
+        def _():
             finish(pair_at(j - 1))
 
-        subs = pair_at(j)
-        f, w = weigh(subs)
-        row_part(subs, f, w)
-        colacc[...] += dot3(split(w.T), split(f), 1, 0)
-        tacc[...] += jnp.broadcast_to(jnp.sum(w, axis=0, keepdims=True), tacc.shape)
         return carry
 
     lax.fori_loop(0, pairs, step, 0)
@@ -356,10 +408,8 @@
         lax.fori_loop(by_place(need, pairs + s - 1), by_place(need, pairs + s), slot, 0)
         if s:
             finish([late[s - 1]])
-        f, w = weigh([late[s]])
+        w = gram([late[s]]) * lkern[s * UR:(s + 1) * UR, :]
         wlate[:, s * UR:(s + 1) * UR] = w.T
-        for core in range(2):
-            lfeat[me_r, s, core] = f[core * hr:(core + 1) * hr, :]
         if s == LATE - 1:
             def push_w(p, carry):
                 to = (me_r + p) % R
@@ -368,11 +418,12 @@
 
             lax.fori_loop(1, R, push_w, 0)
             wlin[me_r] = wlate[at(me_r * NC, NC, 8), :]
-        row_part([late[s]], f, w)
+        row_part([late[s]], rows[0, at(late[s] * UR, UR, 8), :], w)
 
     landed(lfeat.at[pl.ds(0, R - 1), :, 0], pass_in)
     behind = split(lfeat[...].reshape(R * LATE * UR, F))
     finish([late[LATE - 1]])
+    collect()
     landed(colr.at[pl.ds(0, R - 1)], grad_in)
     mine = at(me_r * NC, NC, 8)
     gc_out[...] = colacc[mine, :]
@@ -386,11 +437,19 @@
     w = jnp.concatenate([wlin[p] for p in range(R)], axis=1)
     gc_out[...] += grad_scale * (dot3(split(w), behind, 1, 0) - jnp.sum(w, axis=1, keepdims=True) * cols[0, mine, :])
 
-    landed(rgbuf.at[pl.ds(0, Z - 1)], row_in)
-    total = rgbuf[0]
-    for zs in range(1, Z):
-        total = total + rgbuf[zs]
-    gr_out[...] = total
+    for end in (0, Z - 1):
+        @pl.when(z == end)
+        def _():
+            landed(inbox.at[pl.ds(0, 1)], bulk.at[0])
+            gr_out[...] = inbox[end] + inbox[inward(end)]
+
+    @pl.when(jnp.logical_and(z > 0, z < Z - 1))
+    def _():
+        landed(inbox.at[pl.ds(0, Z - 1)], bulk.at[0])
+        total = inbox[0]
+        for zs in range(1, Z):
+            total = total + inbox[zs]
+        gr_out[...] = total
 
     for d in range(2):
         for y in range(Z - 1):
@@ -402,7 +461,7 @@
     if square:
         landed(cols.at[:, pl.ds(0, NC), :], relay_sent)
     landed(sibp, x_sent)
-    landed(rgbuf.at[pl.ds(0, Z - 1)], row_sent)
+    landed(inbox.at[pl.ds(0, Z - 1)], row_sent)
     landed(colr.at[pl.ds(0, R - 1)], grad_sent)
     landed(wlin.at[pl.ds(0, R - 1)], w_sent)
     landed(lfeat.at[pl.ds(0, R - 1), :, 0], feat_sent)
@@ -447,11 +506,11 @@
             scratch_shapes=[
                 V((Q, C * NR, F), f32), V((Q, R * NC, F), f32),
                 V((Q, R * NC, F), bf16), V((Q, R * NC, F), bf16),
-                V((8, R * NC), f32),
-                V((C * NR, F), f32), V((subs, hr, F), f32), V((subs, hr, F), f32), V((Z, NR, F), f32),
+                V((R * NC, F), bf16), V((8, R * NC), f32),
+                V((C * NR, F), f32), V((subs, hr, F), f32), V((subs, hr, F), f32), V((3 * Z, NR, F), f32), V((2, NR, F), f32),
                 V((R * NC, F), f32), V((8, R * NC), f32), V((R, NC, F), f32),
-                V((R, LATE, 2, hr, F), f32), V((R * NC, LATE * 2 * hr), f32), V((R, NC, LATE * 2 * hr), f32),
-                D((3,)), D((Z, n)), D((subs,)), D((2, Q)), D((subs,)), D((11,)), D((6,)),
+                V((R, LATE, 2, hr, F), f32), V((LATE * 2 * hr, R * NC), f32), V((R * NC, LATE * 2 * hr), f32), V((R, NC, LATE * 2 * hr), f32),
+                D((3,)), D((Z, n)), D((subs, 2)), D((2, Q)), D((subs,)), D((11,)), D((7,)),
             ],
             compiler_params=pltpu.CompilerParams(
                 collective_id=0, has_side_effects=True, vmem_limit_bytes=56 * 1024 * 1024),

time: 45.8 us -> 47 us (1.026)
  Pallas kernels: 44.9 us -> 46.2 us
    pallas_call x1, Pallas kernels: 44 us -> 45.3 us  [local(): pl.pallas_call(functools.partial(kernel, R, C), out_shape=tuple((pltpu.VM...]
where the time goes in v2:
time: 47 us; the launch traced here: 46.8 us
  Pallas kernels  46.2 us (98%)
  between operations  0.64 us (1%)
    pallas_call x1, Pallas kernels, local(): pl.pallas_call(functools.partial(kernel, R, C), out_shape=tuple((pltpu.VM...  45.3 us

profile of v2, /device:TPU:0, one launch (start us, length us, event | category | flops | bytes accessed | tf_op | source)
XLA Modules:
  0.0 46.8 jit_solution(16196345498449235014)
XLA Ops:
  0.6 45.3 %shard_map.76 = (f32[512,256]{1,0:T(8,128)S(1)}, f32[64,512]{1,0:T(8,128)S(1)}, f32[64,512]{1,0:T(8,128)S(1)}) custom-call(f32[64,512]{1,0:T(8,128)} %fr.1, f32[64,512]{1,0:T(8,128)} %fc.1, f32[64,1024]{1,0:T(8,128)} %pr.1, f32[64,1024]{1,0:T(8,128)} %pc.1, f32[512,256]{1,0:T(8,128)} %acc.1), custom_call_target="tpu_custom_call" | custom-call | tf_op jit(solution)/shard_map/pallas_call | solution.py:501
  45.9 0.9 %shard_map.77 = (f32[512,256]{1,0:T(8,128)}, f32[64,512]{1,0:T(8,128)}, f32[64,512]{1,0:T(8,128)}) custom-call(f32[512,256]{1,0:T(8,128)S(1)} %get-tuple-element.6.a, f32[64,512]{1,0:T(8,128)S(1)} %get-tuple-element.7.b, f32[64,512]{1,0:T(8,128)S(1)} %get-tuple-element.8.c), custom_call_target="tpu_custom_call" | custom-call | tf_op jit(solution)/shard_map/pallas_call | solution.py:519

commit v3 on v2

--- a/solution.py
+++ b/solution.py
@@ -32,13 +32,6 @@
     rest = x - hi.astype(jnp.float32)
     mid = rest.astype(jnp.bfloat16)
     return hi, mid, (rest - mid.astype(jnp.float32)).astype(jnp.bfloat16)
-
-
-def dot6(a, b, ca, cb):
-    dims = (((ca,), (cb,)), ((), ()))
-    f = functools.partial(lax.dot_general, dimension_numbers=dims, preferred_element_type=jnp.float32)
-    low = f(a[0], b[2]) + (f(a[2], b[0]) + f(a[1], b[1]))
-    return f(a[0], b[0]) + ((f(a[0], b[1]) + f(a[1], b[0])) + low)
 
 
 def order(n, depth, y, t):
@@ -80,12 +73,12 @@
         subs = own + far if end else far + own
         total = n * max(z, depth - 1 - z)
         late = max(ready(n, depth, z, s, (h * Q,)) for s, h in subs[-LATE:])
-        first = min(total, max(late, n + LEAD - 1))
-        early.append((first, first if end else max(first, total - 1)))
+        first = min(total, max(late, n + LEAD - 2))
+        early.append((first,))
         taken, row = first if end else total, []
         for j, step in enumerate(steps):
             taken = max(taken, min(total, max(at[subs[i]] for i in step) + 1) if j else taken)
-            row.append(taken)
+            row.append(taken if len(step) > 1 else total)
         table.append([s * HALVES + h for s, h in subs])
         need.append(row)
     return table, need, early
@@ -99,7 +92,7 @@
 
 
 def kernel(R, C, fr, fc, pr, pc, acc, accv, gr_out, gc_out,
-           rows, cols, chi, clo, cend, ncol, rowp, sibp, sumb, inbox, csum, colacc, tacc, colr, lfeat, lkern, wlate, wlin,
+           rows, cols, chi, clo, ncol, rowp, sibp, sumb, inbox, csum, colacc, tacc, colr, lfeat, wlate, wlin,
            lsem, rrecv, srecv, crecv, xrecv, sends, bulk):
     me_r, me_c = lax.axis_index("row"), lax.axis_index("col")
     z, k = me_c // 2, me_c % 2
@@ -119,7 +112,8 @@
     across = R - 1 - me_r
     z_sent, sib_sent, col_sent, relay_sent, x_sent, row_sent, grad_sent, w_sent, feat_sent, pass_sent = (
         sends.at[i] for i in (0, 2, 3, 4, 5, 6, 7, 8, 9, 10))
-    grad_in, w_in, feat_in, pass_in, relay_in = (bulk.at[i] for i in range(2, 7))
+    row_in, grad_in, w_in, feat_in, pass_in, relay_in = (bulk.at[i] for i in range(6))
+    half_in = 6
 
     def at(start, size, mult):
         return pl.ds(pl.multiple_of(start, mult), size)
@@ -150,7 +144,7 @@
 
     def scopy(zs, i, src=None):
         dst = rchunk(zs, k, i)
-        return remote(dst if src is None else src, dst, sib_sent, srecv.at[zs * HALVES + i // Q, min(i % Q, 1) if isinstance(i, int) else (i % Q > 0).astype(jnp.int32)], sibling)
+        return remote(dst if src is None else src, dst, sib_sent, srecv.at[zs * HALVES + i // Q], sibling)
 
     for q in range(Q):
         for h in range(HALVES):
@@ -250,9 +244,9 @@
     passed = 0
     if square:
         for q in range(Q):
-            upto = min(RELAY_SLOTS * (q + 1), min(row[0] for row in early))
-            lax.fori_loop(passed, upto, slot, 0)
-            passed = upto
+            until = min(RELAY_SLOTS * (q + 1), min(row[0] for row in early))
+            lax.fori_loop(passed, until, slot, 0)
+            passed = until
             for axis in range(2):
                 own_arrive(axis, q).wait_recv()
                 relay(axis, q).start()
@@ -278,7 +272,6 @@
         chi[q] = hi
         clo[q] = lo
     feats = cols[0]
-    cend[...] = split3(feats)[2]
     ones = jnp.ones((8, F), jnp.bfloat16)
     ncol[...] = sum(lax.dot_general(
         ones, piece, (((1,), (1,)), ((), ())), preferred_element_type=jnp.float32) for piece in reversed(split3(feats * feats)))
@@ -288,28 +281,21 @@
     def exchange(sub):
         return remote(rowp.at[at(sub * UR + (1 - k) * hr, hr, 8), :], sibp.at[sub], x_sent, xrecv.at[sub], sibling)
 
-    def take(subs, q):
+    def weigh(subs):
         for sub in subs:
-            landed(rows.at[:Q - 1 if q else 1, pl.ds(0, hr), :], srecv.at[sub, min(q, 1)])
-
-    def kern(subs):
-        take(subs, 0)
-        f = jnp.concatenate([rows[0, at(sub * UR, UR, 8), :] for sub in subs], axis=0)
-        pieces = split3(f)
-        cross = dot6(pieces, (chi[0], clo[0], cend[...]), 1, 1)
-        dist = jnp.sum(f * f, axis=1, keepdims=True) + ncol[0:1, :] - 2.0 * cross
-        return f, pieces, jnp.exp(-decay_rate * dist)
-
-    def gram(subs):
-        take(subs, 1)
+            landed(rows.at[:, pl.ds(0, hr), :], srecv.at[sub])
+        blocks = [at(sub * UR, UR, 8) for sub in subs]
         parts = [at((2 * (sub // HALVES) + core) * NR + sub % HALVES * hr, hr, 8) for sub in subs for core in range(2)]
+        f = jnp.concatenate([rows[0, b, :] for b in blocks], axis=0)
+        cross = lax.dot_general(f, cols[0], (((1,), (1,)), ((), ())), precision=lax.Precision.HIGHEST, preferred_element_type=jnp.float32)
         g = jnp.concatenate([accv[b, :] for b in parts], axis=0)
         for q in range(1, Q):
-            panel = jnp.concatenate([rows[q, at(sub * UR, UR, 8), :] for sub in subs], axis=0)
+            panel = jnp.concatenate([rows[q, b, :] for b in blocks], axis=0)
             g = g + dot3(split(panel), (chi[q], clo[q]), 1, 1)
         for i, b in enumerate(parts):
             accv[b, :] = g[i * hr:(i + 1) * hr, :]
-        return g
+        dist = jnp.sum(f * f, axis=1, keepdims=True) + ncol[0:1, :] - 2.0 * cross
+        return f, g * jnp.exp(-decay_rate * dist)
 
     def row_part(subs, f, w):
         s = jnp.sum(w, axis=1, keepdims=True)
@@ -328,7 +314,8 @@
             zs, h = sub // HALVES, sub % HALVES
             total = rowp[at(sub * UR + k * hr, hr, 8), :] + sibp[sub]
             own = zs == z
-            group = jnp.where(own, 0, jnp.where(zs == 0, 1, jnp.where(zs == Z - 1, 2, 0)))
+            straight = jnp.logical_or(own, zs == Z - 1 - z)
+            group = jnp.where(straight, 0, jnp.where(zs == 0, 1, jnp.where(zs == Z - 1, 2, 0)))
             to = jnp.where(group == 0, zs, jnp.where(group == 1, inward(0), inward(1)))
             dst = inbox.at[group * Z + z, at(h * hr, hr, 8), :]
 
@@ -339,42 +326,44 @@
             @pl.when(to != z)
             def _():
                 sumb[sub] = total
-                remote(sumb.at[sub], dst, row_sent, bulk.at[jnp.minimum(group, 1)], (me_r, 2 * to + k)).start()
+                got = bulk.at[jnp.where(group > 0, half_in + h, 0)]
+                remote(sumb.at[sub], dst, row_sent, got, (me_r, 2 * to + k)).start()
 
     def collect():
         for e, end in enumerate((0, Z - 1)):
             @pl.when(jnp.logical_and(z == inward(end), z != end))
             def _():
-                if Z > 2:
-                    landed(inbox.at[pl.ds(0, Z - 2)], bulk.at[1])
-                terms = [inbox[(e + 1) * Z + zs] for zs in range(Z) if zs != end]
-                csum[e] = sum(terms[1:], terms[0])
-                remote(csum.at[e], inbox.at[z], row_sent, bulk.at[0], (me_r, 2 * end + k)).start()
+                for h in range(HALVES):
+                    part = pl.ds(h * hr, hr)
+                    if Z > 3:
+                        landed(inbox.at[pl.ds(0, Z - 3), part, :], bulk.at[half_in + h])
+                    terms = [inbox[(e + 1) * Z + zs, part, :] for zs in range(1, Z - 1)]
+                    csum[e, part, :] = sum(terms[1:], terms[0])
+                    remote(csum.at[e, part, :], inbox.at[z, part, :], row_sent, row_in, (me_r, 2 * end + k)).start()
 
     pairs = HALVES * Z // 2 - 1
 
     def pair_at(j):
         return [by_place(table, 2 * j + i) for i in range(2)]
 
-    lax.fori_loop(by_place(early, 0), by_place(early, 1), slot, 0)
-    f, _, weight = kern(late)
-    lkern[...] = weight
-    for s in range(LATE):
-        for core in range(2):
-            lfeat[me_r, s, core] = f[(2 * s + core) * hr:(2 * s + core + 1) * hr, :]
-    lax.fori_loop(by_place(early, 1), by_place(need, 0), slot, 0)
+    lax.fori_loop(by_place(early, 0), by_place(need, 0), slot, 0)
+
+    def upto(a, b):
+        lax.fori_loop(a, b, slot, 0)
+
+    def col_part(f, w):
+        colacc[...] += dot3(split(w.T), split(f), 1, 0)
+        tacc[...] += jnp.broadcast_to(jnp.sum(w, axis=0, keepdims=True), tacc.shape)
 
     def step(j, carry):
         @pl.when(j > 0)
         def _():
-            lax.fori_loop(by_place(need, j - 1), by_place(need, j), slot, 0)
+            upto(by_place(need, j - 1), by_place(need, j))
 
         subs = pair_at(j)
-        f, pieces, weight = kern(subs)
-        w = gram(subs) * weight
+        f, w = weigh(subs)
         row_part(subs, f, w)
-        colacc[...] += dot3(split(w.T), pieces[:2], 1, 0)
-        tacc[...] += jnp.broadcast_to(jnp.sum(w, axis=0, keepdims=True), tacc.shape)
+        col_part(f, w)
 
         @pl.when(j > 0)
         def _():
@@ -382,8 +371,16 @@
 
         return carry
 
-    lax.fori_loop(0, pairs, step, 0)
-
+    lax.fori_loop(0, pairs - 1, step, 0)
+    if pairs > 1:
+        upto(by_place(need, pairs - 2), by_place(need, pairs - 1))
+    final = pair_at(pairs - 1)
+    stops = [by_place(need, pairs - 1)] + [by_place([[row[-1] - 2 + i] for row in need], 0) for i in range(3)]
+    stops = [jnp.maximum(stops[0], stop) for stop in stops]
+    f, w = weigh(final)
+    upto(stops[0], stops[1])
+    row_part(final, f, w)
+    col_part(f, w)
     tcol = jnp.broadcast_to(tacc[0:1, :], (128, tacc.shape[1])).T[:, 0:1]
     colacc[...] = grad_scale * (colacc[...] - tcol * cols[0])
 
@@ -393,7 +390,11 @@
         return carry
 
     lax.fori_loop(1, R, push_grad, 0)
-    finish(pair_at(jnp.int32(pairs - 1)))
+    upto(stops[1], stops[2])
+    if pairs > 1:
+        finish(pair_at(pairs - 2))
+    finish(final)
+    upto(stops[2], stops[3])
 
     landed(lfeat.at[pl.ds(0, R - 1), :, 0], feat_in)
 
@@ -405,11 +406,10 @@
     lax.fori_loop(1, R, pass_on, 0)
 
     for s in range(LATE):
-        lax.fori_loop(by_place(need, pairs + s - 1), by_place(need, pairs + s), slot, 0)
-        if s:
-            finish([late[s - 1]])
-        w = gram([late[s]]) * lkern[s * UR:(s + 1) * UR, :]
+        f, w = weigh([late[s]])
         wlate[:, s * UR:(s + 1) * UR] = w.T
+        for core in range(2):
+            lfeat[me_r, s, core] = f[core * hr:(core + 1) * hr, :]
         if s == LATE - 1:
             def push_w(p, carry):
                 to = (me_r + p) % R
@@ -418,7 +418,8 @@
 
             lax.fori_loop(1, R, push_w, 0)
             wlin[me_r] = wlate[at(me_r * NC, NC, 8), :]
-        row_part([late[s]], rows[0, at(late[s] * UR, UR, 8), :], w)
+        row_part([late[s]], f, w)
+    finish([late[0]])
 
     landed(lfeat.at[pl.ds(0, R - 1), :, 0], pass_in)
     behind = split(lfeat[...].reshape(R * LATE * UR, F))
@@ -440,12 +441,12 @@
     for end in (0, Z - 1):
         @pl.when(z == end)
         def _():
-            landed(inbox.at[pl.ds(0, 1)], bulk.at[0])
-            gr_out[...] = inbox[end] + inbox[inward(end)]
+            landed(inbox.at[pl.ds(0, 2)], row_in)
+            gr_out[...] = inbox[end] + (inbox[inward(end)] + inbox[Z - 1 - end])
 
     @pl.when(jnp.logical_and(z > 0, z < Z - 1))
     def _():
-        landed(inbox.at[pl.ds(0, Z - 1)], bulk.at[0])
+        landed(inbox.at[pl.ds(0, Z - 1)], row_in)
         total = inbox[0]
         for zs in range(1, Z):
             total = total + inbox[zs]
@@ -506,11 +507,11 @@
             scratch_shapes=[
                 V((Q, C * NR, F), f32), V((Q, R * NC, F), f32),
                 V((Q, R * NC, F), bf16), V((Q, R * NC, F), bf16),
-                V((R * NC, F), bf16), V((8, R * NC), f32),
+                V((8, R * NC), f32),
                 V((C * NR, F), f32), V((subs, hr, F), f32), V((subs, hr, F), f32), V((3 * Z, NR, F), f32), V((2, NR, F), f32),
                 V((R * NC, F), f32), V((8, R * NC), f32), V((R, NC, F), f32),
-                V((R, LATE, 2, hr, F), f32), V((LATE * 2 * hr, R * NC), f32), V((R * NC, LATE * 2 * hr), f32), V((R, NC, LATE * 2 * hr), f32),
-                D((3,)), D((Z, n)), D((subs, 2)), D((2, Q)), D((subs,)), D((11,)), D((7,)),
+                V((R, LATE, 2, hr, F), f32), V((R * NC, LATE * 2 * hr), f32), V((R, NC, LATE * 2 * hr), f32),
+                D((3,)), D((Z, n)), D((subs,)), D((2, Q)), D((subs,)), D((11,)), D((8,)),
             ],
             compiler_params=pltpu.CompilerParams(
                 collective_id=0, has_side_effects=True, vmem_limit_bytes=56 * 1024 * 1024),

time: 47 us -> 42.1 us (0.90)
  Pallas kernels: 46.2 us -> 41.3 us
    pallas_call x1, Pallas kernels: 45.3 us -> 40.4 us  [local(): pl.pallas_call(functools.partial(kernel, R, C), out_shape=tuple((pltpu.VM...]
where the time goes in v3:
time: 42.1 us; the launch traced here: 41.9 us
  Pallas kernels  41.3 us (98%)
  between operations  0.64 us (2%)
    pallas_call x1, Pallas kernels, local(): pl.pallas_call(functools.partial(kernel, R, C), out_shape=tuple((pltpu.VM...  40.4 us
    pallas_call x1, Pallas kernels, local(): pl.pallas_call(put, out_shape=tuple((jax.ShapeDtypeStruct(s, f32) for s i...  0.9 us

profile of v3, /device:TPU:0, one launch (start us, length us, event | category | flops | bytes accessed | tf_op | source)
XLA Modules:
  0.0 41.9 jit_solution(5631472784738450166)
XLA Ops:
  0.6 40.4 %shard_map.76 = (f32[512,256]{1,0:T(8,128)S(1)}, f32[64,512]{1,0:T(8,128)S(1)}, f32[64,512]{1,0:T(8,128)S(1)}) custom-call(f32[64,512]{1,0:T(8,128)} %fr.1, f32[64,512]{1,0:T(8,128)} %fc.1, f32[64,1024]{1,0:T(8,128)} %pr.1, f32[64,1024]{1,0:T(8,128)} %pc.1, f32[512,256]{1,0:T(8,128)} %acc.1), custom_call_target="tpu_custom_call" | custom-call | tf_op jit(solution)/shard_map/pallas_call | solution.py:502
  41.0 0.9 %shard_map.77 = (f32[512,256]{1,0:T(8,128)}, f32[64,512]{1,0:T(8,128)}, f32[64,512]{1,0:T(8,128)}) custom-call(f32[512,256]{1,0:T(8,128)S(1)} %get-tuple-element.6.a, f32[64,512]{1,0:T(8,128)S(1)} %get-tuple-element.7.b, f32[64,512]{1,0:T(8,128)S(1)} %get-tuple-element.8.c), custom_call_target="tpu_custom_call" | custom-call | tf_op jit(solution)/shard_map/pallas_call | solution.py:520

commit v4 on v3

--- a/solution.py
+++ b/solution.py
@@ -77,7 +77,7 @@
         early.append((first,))
         taken, row = first if end else total, []
         for j, step in enumerate(steps):
-            taken = max(taken, min(total, max(at[subs[i]] for i in step) + 1) if j else taken)
+            taken = max(taken, min(total, max(at[subs[i]] for i in step)) if j else taken)
             row.append(taken if len(step) > 1 else total)
         table.append([s * HALVES + h for s, h in subs])
         need.append(row)
@@ -92,7 +92,7 @@
 
 
 def kernel(R, C, fr, fc, pr, pc, acc, accv, gr_out, gc_out,
-           rows, cols, chi, clo, ncol, rowp, sibp, sumb, inbox, csum, colacc, tacc, colr, lfeat, wlate, wlin,
+           rows, cols, chi, clo, tall, thi, tlo, ncol, rowp, sibp, sumb, inbox, csum, colacc, tacc, colr, cmid, lfeat, wlate, wlin,
            lsem, rrecv, srecv, crecv, xrecv, sends, bulk):
     me_r, me_c = lax.axis_index("row"), lax.axis_index("col")
     z, k = me_c // 2, me_c % 2
@@ -268,10 +268,17 @@
     lax.fori_loop(1, R, push_late, 0)
 
     for q in range(Q):
-        hi, lo = split(cols[q])
-        chi[q] = hi
-        clo[q] = lo
+        turned = cols[q].T
+        hi, lo = split(turned)
+        if q == 0:
+            tall[...] = turned
+        else:
+            thi[q - 1] = hi
+            tlo[q - 1] = lo
     feats = cols[0]
+    hi, lo = split(feats)
+    chi[...] = hi
+    clo[...] = lo
     ones = jnp.ones((8, F), jnp.bfloat16)
     ncol[...] = sum(lax.dot_general(
         ones, piece, (((1,), (1,)), ((), ())), preferred_element_type=jnp.float32) for piece in reversed(split3(feats * feats)))
@@ -287,11 +294,11 @@
         blocks = [at(sub * UR, UR, 8) for sub in subs]
         parts = [at((2 * (sub // HALVES) + core) * NR + sub % HALVES * hr, hr, 8) for sub in subs for core in range(2)]
         f = jnp.concatenate([rows[0, b, :] for b in blocks], axis=0)
-        cross = lax.dot_general(f, cols[0], (((1,), (1,)), ((), ())), precision=lax.Precision.HIGHEST, preferred_element_type=jnp.float32)
+        cross = lax.dot_general(f, tall[...], (((1,), (0,)), ((), ())), precision=lax.Precision.HIGHEST, preferred_element_type=jnp.float32)
         g = jnp.concatenate([accv[b, :] for b in parts], axis=0)
         for q in range(1, Q):
             panel = jnp.concatenate([rows[q, b, :] for b in blocks], axis=0)
-            g = g + dot3(split(panel), (chi[q], clo[q]), 1, 1)
+            g = g + dot3(split(panel), (thi[q - 1], tlo[q - 1]), 1, 0)
         for i, b in enumerate(parts):
             accv[b, :] = g[i * hr:(i + 1) * hr, :]
         dist = jnp.sum(f * f, axis=1, keepdims=True) + ncol[0:1, :] - 2.0 * cross
@@ -299,7 +306,7 @@
 
     def row_part(subs, f, w):
         s = jnp.sum(w, axis=1, keepdims=True)
-        part = grad_scale * (dot3(split(w), (chi[0], clo[0]), 1, 0) - s * f)
+        part = grad_scale * (dot3(split(w), (chi[...], clo[...]), 1, 0) - s * f)
         for i, sub in enumerate(subs):
             rowp[at(sub * UR, UR, 8), :] = part[i * UR:(i + 1) * UR, :]
         for sub in subs:
@@ -374,11 +381,11 @@
     lax.fori_loop(0, pairs - 1, step, 0)
     if pairs > 1:
         upto(by_place(need, pairs - 2), by_place(need, pairs - 1))
+        finish(pair_at(pairs - 2))
     final = pair_at(pairs - 1)
     stops = [by_place(need, pairs - 1)] + [by_place([[row[-1] - 2 + i] for row in need], 0) for i in range(3)]
     stops = [jnp.maximum(stops[0], stop) for stop in stops]
     f, w = weigh(final)
-    upto(stops[0], stops[1])
     row_part(final, f, w)
     col_part(f, w)
     tcol = jnp.broadcast_to(tacc[0:1, :], (128, tacc.shape[1])).T[:, 0:1]
@@ -389,10 +396,25 @@
         remote(colacc.at[at(to * NC, NC, 8), :], colr.at[me_r], grad_sent, grad_in, (to, me_c)).start()
         return carry
 
-    lax.fori_loop(1, R, push_grad, 0)
-    upto(stops[1], stops[2])
-    if pairs > 1:
-        finish(pair_at(pairs - 2))
+    def half_of(axis):
+        return pl.ds(axis * (F // 2), F // 2)
+
+    def grad_near(axis, half):
+        block = colacc.at[at(near[axis] * NC, NC, 8), half_of(half)]
+        return remote(block, colr.at[axis, :, half_of(half)], grad_sent, grad_in, (near[axis], me_c))
+
+    def grad_across(axis):
+        block = colacc.at[at(across * NC, NC, 8), half_of(axis)]
+        return remote(block, cmid.at[axis], grad_sent, bulk.at[half_in + HALVES + axis], (near[axis], me_c))
+
+    if square:
+        for axis in range(2):
+            grad_across(axis).start()
+        for axis in range(2):
+            grad_near(axis, axis).start()
+    else:
+        lax.fori_loop(1, R, push_grad, 0)
+    upto(stops[0], stops[2])
     finish(final)
     upto(stops[2], stops[3])
 
@@ -419,21 +441,30 @@
             lax.fori_loop(1, R, push_w, 0)
             wlin[me_r] = wlate[at(me_r * NC, NC, 8), :]
         row_part([late[s]], f, w)
+        if s == 0 and square:
+            for axis in range(2):
+                other = 1 - axis
+                grad_across(other).wait_recv()
+                colacc[at(near[axis] * NC, NC, 8), half_of(other)] += cmid[other]
+                grad_near(axis, other).start()
     finish([late[0]])
 
     landed(lfeat.at[pl.ds(0, R - 1), :, 0], pass_in)
     behind = split(lfeat[...].reshape(R * LATE * UR, F))
     finish([late[LATE - 1]])
     collect()
-    landed(colr.at[pl.ds(0, R - 1)], grad_in)
     mine = at(me_r * NC, NC, 8)
-    gc_out[...] = colacc[mine, :]
-
-    def add_grad(p, carry):
-        gc_out[...] += colr[(me_r + p) % R]
-        return carry
-
-    lax.fori_loop(1, R, add_grad, 0)
+    landed(colr.at[pl.ds(0, 2 if square else R - 1)], grad_in)
+    if square:
+        gc_out[...] = colacc[mine, :] + (colr[0] + colr[1])
+    else:
+        gc_out[...] = colacc[mine, :]
+
+        def add_grad(p, carry):
+            gc_out[...] += colr[(me_r + p) % R]
+            return carry
+
+        lax.fori_loop(1, R, add_grad, 0)
     landed(wlin.at[pl.ds(0, R - 1)], w_in)
     w = jnp.concatenate([wlin[p] for p in range(R)], axis=1)
     gc_out[...] += grad_scale * (dot3(split(w), behind, 1, 0) - jnp.sum(w, axis=1, keepdims=True) * cols[0, mine, :])
@@ -506,12 +537,13 @@
             out_specs=(vmem,) * 3,
             scratch_shapes=[
                 V((Q, C * NR, F), f32), V((Q, R * NC, F), f32),
-                V((Q, R * NC, F), bf16), V((Q, R * NC, F), bf16),
+                V((R * NC, F), bf16), V((R * NC, F), bf16), V((F, R * NC), f32),
+                V((Q - 1, F, R * NC), bf16), V((Q - 1, F, R * NC), bf16),
                 V((8, R * NC), f32),
                 V((C * NR, F), f32), V((subs, hr, F), f32), V((subs, hr, F), f32), V((3 * Z, NR, F), f32), V((2, NR, F), f32),
-                V((R * NC, F), f32), V((8, R * NC), f32), V((R, NC, F), f32),
+                V((R * NC, F), f32), V((8, R * NC), f32), V((R, NC, F), f32), V((2, NC, F // 2), f32),
                 V((R, LATE, 2, hr, F), f32), V((R * NC, LATE * 2 * hr), f32), V((R, NC, LATE * 2 * hr), f32),
-                D((3,)), D((Z, n)), D((subs,)), D((2, Q)), D((subs,)), D((11,)), D((8,)),
+                D((3,)), D((Z, n)), D((subs,)), D((2, Q)), D((subs,)), D((11,)), D((10,)),
             ],
             compiler_params=pltpu.CompilerParams(
                 collective_id=0, has_side_effects=True, vmem_limit_bytes=56 * 1024 * 1024),

time: 42.1 us -> 40.6 us (0.964)
  Pallas kernels: 41.3 us -> 39.8 us
    pallas_call x1, Pallas kernels: 40.4 us -> 38.9 us  [local(): pl.pallas_call(functools.partial(kernel, R, C), out_shape=tuple((pltpu.VM...]
where the time goes in v4:
time: 40.6 us; the launch traced here: 40.4 us
  Pallas kernels  39.8 us (98%)
  between operations  0.64 us (2%)
    pallas_call x1, Pallas kernels, local(): pl.pallas_call(functools.partial(kernel, R, C), out_shape=tuple((pltpu.VM...  38.9 us
    pallas_call x1, Pallas kernels, local(): pl.pallas_call(put, out_shape=tuple((jax.ShapeDtypeStruct(s, f32) for s i...  0.9 us

profile of v4, /device:TPU:0, one launch (start us, length us, event | category | flops | bytes accessed | tf_op | source)
XLA Modules:
  0.0 40.4 jit_solution(1879775012782856860)
XLA Ops:
  0.6 38.9 %shard_map.76 = (f32[512,256]{1,0:T(8,128)S(1)}, f32[64,512]{1,0:T(8,128)S(1)}, f32[64,512]{1,0:T(8,128)S(1)}) custom-call(f32[64,512]{1,0:T(8,128)} %fr.1, f32[64,512]{1,0:T(8,128)} %fc.1, f32[64,1024]{1,0:T(8,128)} %pr.1, f32[64,1024]{1,0:T(8,128)} %pc.1, f32[512,256]{1,0:T(8,128)} %acc.1), custom_call_target="tpu_custom_call" | custom-call | tf_op jit(solution)/shard_map/pallas_call | solution.py:533
  39.5 0.9 %shard_map.77 = (f32[512,256]{1,0:T(8,128)}, f32[64,512]{1,0:T(8,128)}, f32[64,512]{1,0:T(8,128)}) custom-call(f32[512,256]{1,0:T(8,128)S(1)} %get-tuple-element.6.a, f32[64,512]{1,0:T(8,128)S(1)} %get-tuple-element.7.b, f32[64,512]{1,0:T(8,128)S(1)} %get-tuple-element.8.c), custom_call_target="tpu_custom_call" | custom-call | tf_op jit(solution)/shard_map/pallas_call | solution.py:552

commit v5 on v4

--- a/solution.py
+++ b/solution.py
@@ -14,6 +14,7 @@
 LEAD = 4
 RELAY_SLOTS = 2
 LATE = 2
+PIECES = 4
 
 
 def split(x):
@@ -68,8 +69,8 @@
         own = [(z, h) for h in range(HALVES)]
         far = [(s, h) for s in range(depth) for h in range(HALVES) if s != z]
         at = {(s, h): ready(n, depth, z, s, range(h * Q, h * Q + Q)) for s, h in own + far}
-        far = sorted(far, key=lambda u: (at[u], -abs(u[0] - z)))
         end = z in (0, depth - 1)
+        far = sorted(far, key=lambda u: (at[u], -abs(u[0] - z)) if end else (u[0] not in (0, depth - 1),))
         subs = own + far if end else far + own
         total = n * max(z, depth - 1 - z)
         late = max(ready(n, depth, z, s, (h * Q,)) for s, h in subs[-LATE:])
@@ -92,7 +93,7 @@
 
 
 def kernel(R, C, fr, fc, pr, pc, acc, accv, gr_out, gc_out,
-           rows, cols, chi, clo, tall, thi, tlo, ncol, rowp, sibp, sumb, inbox, csum, colacc, tacc, colr, cmid, lfeat, wlate, wlin,
+           rows, cols, chi, clo, tall, thi, tlo, ncol, rowp, sibp, sumb, inbox, csum, colacc, colr, cmid, lfeat, wlate, wlin,
            lsem, rrecv, srecv, crecv, xrecv, sends, bulk):
     me_r, me_c = lax.axis_index("row"), lax.axis_index("col")
     z, k = me_c // 2, me_c % 2
@@ -110,8 +111,7 @@
     square = R == 4
     near = (me_r // 2 * 2 + 1 - me_r % 2, (1 - me_r // 2) * 2 + me_r % 2)
     across = R - 1 - me_r
-    z_sent, sib_sent, col_sent, relay_sent, x_sent, row_sent, grad_sent, w_sent, feat_sent, pass_sent = (
-        sends.at[i] for i in (0, 2, 3, 4, 5, 6, 7, 8, 9, 10))
+    sent = sends.at[2]
     row_in, grad_in, w_in, feat_in, pass_in, relay_in = (bulk.at[i] for i in range(6))
     half_in = 6
 
@@ -144,8 +144,23 @@
 
     def scopy(zs, i, src=None):
         dst = rchunk(zs, k, i)
-        return remote(dst if src is None else src, dst, sib_sent, srecv.at[zs * HALVES + i // Q], sibling)
-
+        return remote(dst if src is None else src, dst, sent, srecv.at[zs * HALVES + i // Q], sibling)
+
+    barrier = pltpu.get_barrier_semaphore()
+    if square:
+        for axis in range(2):
+            pl.semaphore_signal(barrier, inc=1, device_id=(near[axis], me_c), device_id_type=MESH)
+    else:
+        def greet(p, carry):
+            pl.semaphore_signal(barrier, inc=1, device_id=((me_r + p) % R, me_c), device_id_type=MESH)
+            return carry
+
+        lax.fori_loop(1, R, greet, 0)
+    pl.semaphore_signal(barrier, inc=1, device_id=sibling, device_id_type=MESH)
+    for d in range(2):
+        @pl.when(place[d] < Z - 1)
+        def _():
+            pl.semaphore_signal(barrier, inc=1, device_id=(me_r, me_c + step_to[d]), device_id_type=MESH)
     for q in range(Q):
         for h in range(HALVES):
             pltpu.make_async_copy(own_chunk(h * Q + q), rchunk(z, k, h * Q + q), lsem.at[0]).start()
@@ -153,21 +168,6 @@
     acc_in = pltpu.make_async_copy(acc, accv, lsem.at[2])
     acc_in.start()
 
-    barrier = pltpu.get_barrier_semaphore()
-    if square:
-        for axis in range(2):
-            pl.semaphore_signal(barrier, inc=1, device_id=(near[axis], me_c), device_id_type=MESH)
-    else:
-        def greet(p, carry):
-            pl.semaphore_signal(barrier, inc=1, device_id=((me_r + p) % R, me_c), device_id_type=MESH)
-            return carry
-
-        lax.fori_loop(1, R, greet, 0)
-    pl.semaphore_signal(barrier, inc=1, device_id=sibling, device_id_type=MESH)
-    for d in range(2):
-        @pl.when(place[d] < Z - 1)
-        def _():
-            pl.semaphore_signal(barrier, inc=1, device_id=(me_r, me_c + step_to[d]), device_id_type=MESH)
     greeted = (2 if square else R - 1) + 1
     pl.semaphore_wait(barrier, greeted + (z > 0).astype(jnp.int32) + (z < Z - 1).astype(jnp.int32))
 
@@ -182,20 +182,20 @@
 
     def own_push(axis, q):
         block = cols.at[q, at(me_r * NC, NC, 8), :]
-        return remote(own_cols(q), block, col_sent, crecv.at[axis, q], (near[axis], me_c))
+        return remote(own_cols(q), block, sent, crecv.at[axis, q], (near[axis], me_c))
 
     def own_arrive(axis, q):
         block = cols.at[q, at(near[axis] * NC, NC, 8), :]
-        return remote(block, block, col_sent, crecv.at[axis, q], (near[axis], me_c))
+        return remote(block, block, sent, crecv.at[axis, q], (near[axis], me_c))
 
     def relay(axis, q):
         block = cols.at[q, at(near[axis] * NC + axis * (NC // 2), NC // 2, 8), :]
-        return remote(block, block, relay_sent, relay_in, (near[1 - axis], me_c))
+        return remote(block, block, sent, relay_in, (near[1 - axis], me_c))
 
     def push_cols(p, carry):
         for q in range(Q):
             block = cols.at[q, at(me_r * NC, NC, 8), :]
-            remote(own_cols(q), block, col_sent, relay_in, ((me_r + p) % R, me_c)).start()
+            remote(own_cols(q), block, sent, relay_in, ((me_r + p) % R, me_c)).start()
         return carry
 
     if square:
@@ -262,7 +262,7 @@
     def push_late(p, carry):
         for s in range(LATE):
             src = rows.at[0, at(late[s] * UR + k * hr, hr, 8), :]
-            remote(src, lfeat.at[me_r, s, k], feat_sent, feat_in, ((me_r + p) % R, me_c)).start()
+            remote(src, lfeat.at[me_r, s, k], sent, feat_in, ((me_r + p) % R, me_c)).start()
         return carry
 
     lax.fori_loop(1, R, push_late, 0)
@@ -283,10 +283,9 @@
     ncol[...] = sum(lax.dot_general(
         ones, piece, (((1,), (1,)), ((), ())), preferred_element_type=jnp.float32) for piece in reversed(split3(feats * feats)))
     colacc[...] = jnp.zeros_like(colacc)
-    tacc[...] = jnp.zeros_like(tacc)
 
     def exchange(sub):
-        return remote(rowp.at[at(sub * UR + (1 - k) * hr, hr, 8), :], sibp.at[sub], x_sent, xrecv.at[sub], sibling)
+        return remote(rowp.at[at(sub * UR + (1 - k) * hr, hr, 8), :], sibp.at[sub], sent, xrecv.at[sub], sibling)
 
     def weigh(subs):
         for sub in subs:
@@ -334,7 +333,7 @@
             def _():
                 sumb[sub] = total
                 got = bulk.at[jnp.where(group > 0, half_in + h, 0)]
-                remote(sumb.at[sub], dst, row_sent, got, (me_r, 2 * to + k)).start()
+                remote(sumb.at[sub], dst, sent, got, (me_r, 2 * to + k)).start()
 
     def collect():
         for e, end in enumerate((0, Z - 1)):
@@ -346,7 +345,7 @@
                         landed(inbox.at[pl.ds(0, Z - 3), part, :], bulk.at[half_in + h])
                     terms = [inbox[(e + 1) * Z + zs, part, :] for zs in range(1, Z - 1)]
                     csum[e, part, :] = sum(terms[1:], terms[0])
-                    remote(csum.at[e, part, :], inbox.at[z, part, :], row_sent, row_in, (me_r, 2 * end + k)).start()
+                    remote(csum.at[e, part, :], inbox.at[z, part, :], sent, row_in, (me_r, 2 * end + k)).start()
 
     pairs = HALVES * Z // 2 - 1
 
@@ -359,8 +358,9 @@
         lax.fori_loop(a, b, slot, 0)
 
     def col_part(f, w):
-        colacc[...] += dot3(split(w.T), split(f), 1, 0)
-        tacc[...] += jnp.broadcast_to(jnp.sum(w, axis=0, keepdims=True), tacc.shape)
+        turned = w.T
+        part = dot3(split(turned), split(f), 1, 0)
+        colacc[...] += grad_scale * (part - jnp.sum(turned, axis=1, keepdims=True) * cols[0])
 
     def step(j, carry):
         @pl.when(j > 0)
@@ -388,12 +388,10 @@
     f, w = weigh(final)
     row_part(final, f, w)
     col_part(f, w)
-    tcol = jnp.broadcast_to(tacc[0:1, :], (128, tacc.shape[1])).T[:, 0:1]
-    colacc[...] = grad_scale * (colacc[...] - tcol * cols[0])
 
     def push_grad(p, carry):
         to = (me_r + p) % R
-        remote(colacc.at[at(to * NC, NC, 8), :], colr.at[me_r], grad_sent, grad_in, (to, me_c)).start()
+        remote(colacc.at[at(to * NC, NC, 8), :], colr.at[me_r], sent, grad_in, (to, me_c)).start()
         return carry
 
     def half_of(axis):
@@ -401,28 +399,29 @@
 
     def grad_near(axis, half):
         block = colacc.at[at(near[axis] * NC, NC, 8), half_of(half)]
-        return remote(block, colr.at[axis, :, half_of(half)], grad_sent, grad_in, (near[axis], me_c))
+        return remote(block, colr.at[axis, :, half_of(half)], sent, grad_in, (near[axis], me_c))
 
     def grad_across(axis):
         block = colacc.at[at(across * NC, NC, 8), half_of(axis)]
-        return remote(block, cmid.at[axis], grad_sent, bulk.at[half_in + HALVES + axis], (near[axis], me_c))
+        return remote(block, cmid.at[axis], sent, bulk.at[half_in + HALVES + axis], (near[axis], me_c))
 
     if square:
         for axis in range(2):
             grad_across(axis).start()
-        for axis in range(2):
-            grad_near(axis, axis).start()
     else:
         lax.fori_loop(1, R, push_grad, 0)
     upto(stops[0], stops[2])
     finish(final)
+    if square:
+        for axis in range(2):
+            grad_near(axis, axis).start()
     upto(stops[2], stops[3])
 
     landed(lfeat.at[pl.ds(0, R - 1), :, 0], feat_in)
 
     def pass_on(p, carry):
         block = lfeat.at[(me_r + p) % R, :, k]
-        remote(block, block, pass_sent, pass_in, sibling).start()
+        remote(block, block, sent, pass_in, sibling).start()
         return carry
 
     lax.fori_loop(1, R, pass_on, 0)
@@ -435,24 +434,25 @@
         if s == LATE - 1:
             def push_w(p, carry):
                 to = (me_r + p) % R
-                remote(wlate.at[at(to * NC, NC, 8), :], wlin.at[me_r], w_sent, w_in, (to, me_c)).start()
+                remote(wlate.at[at(to * NC, NC, 8), :], wlin.at[me_r], sent, w_in, (to, me_c)).start()
                 return carry
 
             lax.fori_loop(1, R, push_w, 0)
             wlin[me_r] = wlate[at(me_r * NC, NC, 8), :]
         row_part([late[s]], f, w)
+        if s == 0:
+            collect()
         if s == 0 and square:
             for axis in range(2):
                 other = 1 - axis
                 grad_across(other).wait_recv()
                 colacc[at(near[axis] * NC, NC, 8), half_of(other)] += cmid[other]
                 grad_near(axis, other).start()
-    finish([late[0]])
-
+        if s == 0:
+            finish([late[0]])
     landed(lfeat.at[pl.ds(0, R - 1), :, 0], pass_in)
     behind = split(lfeat[...].reshape(R * LATE * UR, F))
     finish([late[LATE - 1]])
-    collect()
     mine = at(me_r * NC, NC, 8)
     landed(colr.at[pl.ds(0, 2 if square else R - 1)], grad_in)
     if square:
@@ -488,20 +488,22 @@
             @pl.when(place[d] == y)
             def _():
                 landed(rows.at[:, pl.ds(0, (y + 1) * NR), :], sends.at[d])
-    landed(rows.at[:, pl.ds(0, Z * NR), :], sib_sent)
-    landed(cols.at[:, pl.ds(0, (2 if square else R - 1) * NC), :], col_sent)
-    if square:
-        landed(cols.at[:, pl.ds(0, NC), :], relay_sent)
-    landed(sibp, x_sent)
-    landed(inbox.at[pl.ds(0, Z - 1)], row_sent)
-    landed(colr.at[pl.ds(0, R - 1)], grad_sent)
-    landed(wlin.at[pl.ds(0, R - 1)], w_sent)
-    landed(lfeat.at[pl.ds(0, R - 1), :, 0], feat_sent)
-    landed(lfeat.at[pl.ds(0, R - 1), :, 0], pass_sent)
+    landed(rows.at[:, pl.ds(0, Z * NR), :], sent)
+    landed(cols.at[:, pl.ds(0, (2 if square else R - 1) * NC), :], sent)
+    if square:
+        landed(cols.at[:, pl.ds(0, NC), :], sent)
+    landed(sibp, sent)
+    landed(inbox.at[pl.ds(0, Z - 1)], sent)
+    landed(colr.at[pl.ds(0, R - 1)], sent)
+    landed(wlin.at[pl.ds(0, R - 1)], sent)
+    landed(lfeat.at[pl.ds(0, R - 1), :, 0], sent)
+    landed(lfeat.at[pl.ds(0, R - 1), :, 0], sent)
 
 
 def put(a, b, c, x, y, w, sem):
-    copies = [pltpu.make_async_copy(u, v, sem.at[i]) for i, (u, v) in enumerate(((a, x), (b, y), (c, w)))]
+    size = a.shape[0] // PIECES
+    parts = [(a.at[pl.ds(i * size, size), :], x.at[pl.ds(i * size, size), :]) for i in range(PIECES)]
+    copies = [pltpu.make_async_copy(u, v, sem.at[i]) for i, (u, v) in enumerate(parts + [(b, y), (c, w)])]
     for copy in copies:
         copy.start()
     for copy in copies:
@@ -541,9 +543,9 @@
                 V((Q - 1, F, R * NC), bf16), V((Q - 1, F, R * NC), bf16),
                 V((8, R * NC), f32),
                 V((C * NR, F), f32), V((subs, hr, F), f32), V((subs, hr, F), f32), V((3 * Z, NR, F), f32), V((2, NR, F), f32),
-                V((R * NC, F), f32), V((8, R * NC), f32), V((R, NC, F), f32), V((2, NC, F // 2), f32),
+                V((R * NC, F), f32), V((R, NC, F), f32), V((2, NC, F // 2), f32),
                 V((R, LATE, 2, hr, F), f32), V((R * NC, LATE * 2 * hr), f32), V((R, NC, LATE * 2 * hr), f32),
-                D((3,)), D((Z, n)), D((subs,)), D((2, Q)), D((subs,)), D((11,)), D((10,)),
+                D((3,)), D((Z, n)), D((subs,)), D((2, Q)), D((subs,)), D((3,)), D((10,)),
             ],
             compiler_params=pltpu.CompilerParams(
                 collective_id=0, has_side_effects=True, vmem_limit_bytes=56 * 1024 * 1024),
@@ -554,7 +556,7 @@
             out_shape=tuple(jax.ShapeDtypeStruct(s, f32) for s in shapes),
             in_specs=[vmem] * 3,
             out_specs=(hbm,) * 3,
-            scratch_shapes=[D((3,))],
+            scratch_shapes=[D((PIECES + 2,))],
         )(*made)
         return tuple(done)
 

time: 40.6 us -> 40 us (0.985)
  Pallas kernels: 39.8 us -> 39.2 us
    pallas_call x1, Pallas kernels: 38.9 us -> 38.3 us  [local(): pl.pallas_call(functools.partial(kernel, R, C), out_shape=tuple((pltpu.VM...]
where the time goes in v5:
time: 40 us; the launch traced here: 39.8 us
  Pallas kernels  39.2 us (98%)
  between operations  0.64 us (2%)
    pallas_call x1, Pallas kernels, local(): pl.pallas_call(functools.partial(kernel, R, C), out_shape=tuple((pltpu.VM...  38.3 us
    pallas_call x1, Pallas kernels, local(): pl.pallas_call(put, out_shape=tuple((jax.ShapeDtypeStruct(s, f32) for s i...  0.93 us

profile of v5, /device:TPU:0, one launch (start us, length us, event | category | flops | bytes accessed | tf_op | source)
XLA Modules:
  0.0 39.8 jit_solution(17103143823539939950)
XLA Ops:
  0.6 38.3 %shard_map.76 = (f32[512,256]{1,0:T(8,128)S(1)}, f32[64,512]{1,0:T(8,128)S(1)}, f32[64,512]{1,0:T(8,128)S(1)}) custom-call(f32[64,512]{1,0:T(8,128)} %fr.1, f32[64,512]{1,0:T(8,128)} %fc.1, f32[64,1024]{1,0:T(8,128)} %pr.1, f32[64,1024]{1,0:T(8,128)} %pc.1, f32[512,256]{1,0:T(8,128)} %acc.1), custom_call_target="tpu_custom_call" | custom-call | tf_op jit(solution)/shard_map/pallas_call | solution.py:535
  38.9 0.9 %shard_map.77 = (f32[512,256]{1,0:T(8,128)}, f32[64,512]{1,0:T(8,128)}, f32[64,512]{1,0:T(8,128)}) custom-call(f32[512,256]{1,0:T(8,128)S(1)} %get-tuple-element.6.a, f32[64,512]{1,0:T(8,128)S(1)} %get-tuple-element.7.b, f32[64,512]{1,0:T(8,128)S(1)} %get-tuple-element.8.c), custom_call_target="tpu_custom_call" | custom-call | tf_op jit(solution)/shard_map/pallas_call | solution.py:554

commit v6 on v5

--- a/solution.py
+++ b/solution.py
@@ -428,17 +428,20 @@
 
     for s in range(LATE):
         f, w = weigh([late[s]])
-        wlate[:, s * UR:(s + 1) * UR] = w.T
+        turned, half = w.T, NC // 2
+        for p in range(R):
+            wlate[s, p * half:(p + 1) * half, :] = jnp.concatenate(
+                [turned[p * NC + side * half:p * NC + (side + 1) * half, :] for side in range(2)], axis=1)
         for core in range(2):
             lfeat[me_r, s, core] = f[core * hr:(core + 1) * hr, :]
-        if s == LATE - 1:
-            def push_w(p, carry):
-                to = (me_r + p) % R
-                remote(wlate.at[at(to * NC, NC, 8), :], wlin.at[me_r], sent, w_in, (to, me_c)).start()
-                return carry
-
-            lax.fori_loop(1, R, push_w, 0)
-            wlin[me_r] = wlate[at(me_r * NC, NC, 8), :]
+
+        def push_w(p, carry, s=s):
+            to = (me_r + p) % R
+            remote(wlate.at[s, at(to * (NC // 2), NC // 2, 8), :], wlin.at[s, me_r], sent, w_in, (to, me_c)).start()
+            return carry
+
+        lax.fori_loop(1, R, push_w, 0)
+        wlin[s, me_r] = wlate[s, at(me_r * half, half, 8), :]
         row_part([late[s]], f, w)
         if s == 0:
             collect()
@@ -465,8 +468,10 @@
             return carry
 
         lax.fori_loop(1, R, add_grad, 0)
-    landed(wlin.at[pl.ds(0, R - 1)], w_in)
-    w = jnp.concatenate([wlin[p] for p in range(R)], axis=1)
+    landed(wlin.at[:, pl.ds(0, R - 1)], w_in)
+    w = jnp.concatenate([jnp.concatenate(
+        [jnp.concatenate([wlin[s, p, :, side * UR:(side + 1) * UR] for s in range(LATE)], axis=1) for side in range(2)],
+        axis=0) for p in range(R)], axis=1)
     gc_out[...] += grad_scale * (dot3(split(w), behind, 1, 0) - jnp.sum(w, axis=1, keepdims=True) * cols[0, mine, :])
 
     for end in (0, Z - 1):
@@ -495,7 +500,7 @@
     landed(sibp, sent)
     landed(inbox.at[pl.ds(0, Z - 1)], sent)
     landed(colr.at[pl.ds(0, R - 1)], sent)
-    landed(wlin.at[pl.ds(0, R - 1)], sent)
+    landed(wlin.at[:, pl.ds(0, R - 1)], sent)
     landed(lfeat.at[pl.ds(0, R - 1), :, 0], sent)
     landed(lfeat.at[pl.ds(0, R - 1), :, 0], sent)
 
@@ -544,7 +549,7 @@
                 V((8, R * NC), f32),
                 V((C * NR, F), f32), V((subs, hr, F), f32), V((subs, hr, F), f32), V((3 * Z, NR, F), f32), V((2, NR, F), f32),
                 V((R * NC, F), f32), V((R, NC, F), f32), V((2, NC, F // 2), f32),
-                V((R, LATE, 2, hr, F), f32), V((R * NC, LATE * 2 * hr), f32), V((R, NC, LATE * 2 * hr), f32),
+                V((R, LATE, 2, hr, F), f32), V((LATE, R * NC // 2, 4 * hr), f32), V((LATE, R, NC // 2, 4 * hr), f32),
                 D((3,)), D((Z, n)), D((subs,)), D((2, Q)), D((subs,)), D((3,)), D((10,)),
             ],
             compiler_params=pltpu.CompilerParams(

time: 40 us -> 39.8 us (level)
  no operation moved by 1% of the time
where the time goes in v6:
time: 39.8 us; the launch traced here: 39.7 us
  Pallas kernels  39.1 us (98%)
  between operations  0.64 us (2%)
    pallas_call x1, Pallas kernels, local(): pl.pallas_call(functools.partial(kernel, R, C), out_shape=tuple((pltpu.VM...  38.1 us
    pallas_call x1, Pallas kernels, local(): pl.pallas_call(put, out_shape=tuple((jax.ShapeDtypeStruct(s, f32) for s i...  0.93 us

profile of v6, /device:TPU:0, one launch (start us, length us, event | category | flops | bytes accessed | tf_op | source)
XLA Modules:
  0.0 39.7 jit_solution(10720365130126940195)
XLA Ops:
  0.6 38.1 %shard_map.76 = (f32[512,256]{1,0:T(8,128)S(1)}, f32[64,512]{1,0:T(8,128)S(1)}, f32[64,512]{1,0:T(8,128)S(1)}) custom-call(f32[64,512]{1,0:T(8,128)} %fr.1, f32[64,512]{1,0:T(8,128)} %fc.1, f32[64,1024]{1,0:T(8,128)} %pr.1, f32[64,1024]{1,0:T(8,128)} %pc.1, f32[512,256]{1,0:T(8,128)} %acc.1), custom_call_target="tpu_custom_call" | custom-call | tf_op jit(solution)/shard_map/pallas_call | solution.py:540
  38.8 0.9 %shard_map.77 = (f32[512,256]{1,0:T(8,128)}, f32[64,512]{1,0:T(8,128)}, f32[64,512]{1,0:T(8,128)}) custom-call(f32[512,256]{1,0:T(8,128)S(1)} %get-tuple-element.6.a, f32[64,512]{1,0:T(8,128)S(1)} %get-tuple-element.7.b, f32[64,512]{1,0:T(8,128)S(1)} %get-tuple-element.8.c), custom_call_target="tpu_custom_call" | custom-call | tf_op jit(solution)/shard_map/pallas_call | solution.py:559

commit v7 on v6

--- a/solution.py
+++ b/solution.py
@@ -112,8 +112,8 @@
     near = (me_r // 2 * 2 + 1 - me_r % 2, (1 - me_r // 2) * 2 + me_r % 2)
     across = R - 1 - me_r
     sent = sends.at[2]
-    row_in, grad_in, w_in, feat_in, pass_in, relay_in = (bulk.at[i] for i in range(6))
-    half_in = 6
+    row_in, grad_in, feat_in, pass_in, relay_in = (bulk.at[i] for i in range(5))
+    half_in, w_in = 5, bulk.at[pl.ds(5 + HALVES + 2, LATE)]
 
     def at(start, size, mult):
         return pl.ds(pl.multiple_of(start, mult), size)
@@ -138,9 +138,12 @@
     def own_cols(q):
         return fc if q == 0 else pc.at[:, pl.ds((q - 1) * F, F)]
 
+    def far(zs, d):
+        return zs if d == 0 else zs - 1
+
     def zcopy(d, zs, i, src=None):
         dst = rchunk(zs, k, i)
-        return remote(dst if src is None else src, dst, sends.at[d], rrecv.at[zs, i], (me_r, me_c + step_to[d]))
+        return remote(dst if src is None else src, dst, sends.at[d], rrecv.at[far(zs, d), i], (me_r, me_c + step_to[d]))
 
     def scopy(zs, i, src=None):
         dst = rchunk(zs, k, i)
@@ -182,11 +185,7 @@
 
     def own_push(axis, q):
         block = cols.at[q, at(me_r * NC, NC, 8), :]
-        return remote(own_cols(q), block, sent, crecv.at[axis, q], (near[axis], me_c))
-
-    def own_arrive(axis, q):
-        block = cols.at[q, at(near[axis] * NC, NC, 8), :]
-        return remote(block, block, sent, crecv.at[axis, q], (near[axis], me_c))
+        return remote(own_cols(q), block, sent, crecv.at[q], (near[axis], me_c))
 
     def relay(axis, q):
         block = cols.at[q, at(near[axis] * NC + axis * (NC // 2), NC // 2, 8), :]
@@ -247,8 +246,8 @@
             until = min(RELAY_SLOTS * (q + 1), min(row[0] for row in early))
             lax.fori_loop(passed, until, slot, 0)
             passed = until
+            landed(cols.at[q, pl.ds(0, 2 * NC), :], crecv.at[q])
             for axis in range(2):
-                own_arrive(axis, q).wait_recv()
                 relay(axis, q).start()
     lax.fori_loop(passed, by_place(early, 0), slot, 0)
 
@@ -410,12 +409,12 @@
             grad_across(axis).start()
     else:
         lax.fori_loop(1, R, push_grad, 0)
-    upto(stops[0], stops[2])
-    finish(final)
+    upto(stops[0], stops[1])
     if square:
         for axis in range(2):
             grad_near(axis, axis).start()
-    upto(stops[2], stops[3])
+    finish(final)
+    upto(stops[1], stops[3])
 
     landed(lfeat.at[pl.ds(0, R - 1), :, 0], feat_in)
 
@@ -437,14 +436,12 @@
 
         def push_w(p, carry, s=s):
             to = (me_r + p) % R
-            remote(wlate.at[s, at(to * (NC // 2), NC // 2, 8), :], wlin.at[s, me_r], sent, w_in, (to, me_c)).start()
+            remote(wlate.at[s, at(to * (NC // 2), NC // 2, 8), :], wlin.at[s, me_r], sent, w_in.at[s], (to, me_c)).start()
             return carry
 
         lax.fori_loop(1, R, push_w, 0)
         wlin[s, me_r] = wlate[s, at(me_r * half, half, 8), :]
         row_part([late[s]], f, w)
-        if s == 0:
-            collect()
         if s == 0 and square:
             for axis in range(2):
                 other = 1 - axis
@@ -452,27 +449,31 @@
                 colacc[at(near[axis] * NC, NC, 8), half_of(other)] += cmid[other]
                 grad_near(axis, other).start()
         if s == 0:
+            collect()
             finish([late[0]])
     landed(lfeat.at[pl.ds(0, R - 1), :, 0], pass_in)
-    behind = split(lfeat[...].reshape(R * LATE * UR, F))
     finish([late[LATE - 1]])
     mine = at(me_r * NC, NC, 8)
+
+    def late_part(s):
+        landed(wlin.at[s, pl.ds(0, R - 1)], w_in.at[s])
+        w = jnp.concatenate([jnp.concatenate(
+            [wlin[s, p, :, side * UR:(side + 1) * UR] for p in range(R)], axis=1) for side in range(2)], axis=0)
+        there = lfeat[:, s].reshape(R * UR, F)
+        return grad_scale * (dot3(split(w), split(there), 1, 0) - jnp.sum(w, axis=1, keepdims=True) * cols[0, mine, :])
+
+    gc_out[...] = colacc[mine, :] + late_part(0)
     landed(colr.at[pl.ds(0, 2 if square else R - 1)], grad_in)
     if square:
-        gc_out[...] = colacc[mine, :] + (colr[0] + colr[1])
+        gc_out[...] += colr[0] + colr[1]
     else:
-        gc_out[...] = colacc[mine, :]
-
         def add_grad(p, carry):
             gc_out[...] += colr[(me_r + p) % R]
             return carry
 
         lax.fori_loop(1, R, add_grad, 0)
-    landed(wlin.at[:, pl.ds(0, R - 1)], w_in)
-    w = jnp.concatenate([jnp.concatenate(
-        [jnp.concatenate([wlin[s, p, :, side * UR:(side + 1) * UR] for s in range(LATE)], axis=1) for side in range(2)],
-        axis=0) for p in range(R)], axis=1)
-    gc_out[...] += grad_scale * (dot3(split(w), behind, 1, 0) - jnp.sum(w, axis=1, keepdims=True) * cols[0, mine, :])
+    for s in range(1, LATE):
+        gc_out[...] += late_part(s)
 
     for end in (0, Z - 1):
         @pl.when(z == end)
@@ -550,7 +551,7 @@
                 V((C * NR, F), f32), V((subs, hr, F), f32), V((subs, hr, F), f32), V((3 * Z, NR, F), f32), V((2, NR, F), f32),
                 V((R * NC, F), f32), V((R, NC, F), f32), V((2, NC, F // 2), f32),
                 V((R, LATE, 2, hr, F), f32), V((LATE, R * NC // 2, 4 * hr), f32), V((LATE, R, NC // 2, 4 * hr), f32),
-                D((3,)), D((Z, n)), D((subs,)), D((2, Q)), D((subs,)), D((3,)), D((10,)),
+                D((3,)), D((Z - 1, n)), D((subs,)), D((Q,)), D((subs,)), D((3,)), D((9 + LATE,)),
             ],
             compiler_params=pltpu.CompilerParams(
                 collective_id=0, has_side_effects=True, vmem_limit_bytes=56 * 1024 * 1024),

time: 39.8 us -> 39.8 us (level)
  no operation moved by 1% of the time
where the time goes in v7:
time: 39.8 us; the launch traced here: 39.7 us
  Pallas kernels  39 us (98%)
  between operations  0.64 us (2%)
    pallas_call x1, Pallas kernels, local(): pl.pallas_call(functools.partial(kernel, R, C), out_shape=tuple((pltpu.VM...  38.1 us
    pallas_call x1, Pallas kernels, local(): pl.pallas_call(put, out_shape=tuple((jax.ShapeDtypeStruct(s, f32) for s i...  0.93 us

profile of v7, /device:TPU:0, one launch (start us, length us, event | category | flops | bytes accessed | tf_op | source)
XLA Modules:
  0.0 39.7 jit_solution(3648734983941102865)
XLA Ops:
  0.6 38.1 %shard_map.76 = (f32[512,256]{1,0:T(8,128)S(1)}, f32[64,512]{1,0:T(8,128)S(1)}, f32[64,512]{1,0:T(8,128)S(1)}) custom-call(f32[64,512]{1,0:T(8,128)} %fr.1, f32[64,512]{1,0:T(8,128)} %fc.1, f32[64,1024]{1,0:T(8,128)} %pr.1, f32[64,1024]{1,0:T(8,128)} %pc.1, f32[512,256]{1,0:T(8,128)} %acc.1), custom_call_target="tpu_custom_call" | custom-call | tf_op jit(solution)/shard_map/pallas_call | solution.py:541
  38.8 0.9 %shard_map.77 = (f32[512,256]{1,0:T(8,128)}, f32[64,512]{1,0:T(8,128)}, f32[64,512]{1,0:T(8,128)}) custom-call(f32[512,256]{1,0:T(8,128)S(1)} %get-tuple-element.6.a, f32[64,512]{1,0:T(8,128)S(1)} %get-tuple-element.7.b, f32[64,512]{1,0:T(8,128)S(1)} %get-tuple-element.8.c), custom_call_target="tpu_custom_call" | custom-call | tf_op jit(solution)/shard_map/pallas_call | solution.py:560

commit v8 on v7

--- a/solution.py
+++ b/solution.py
@@ -14,7 +14,7 @@
 LEAD = 4
 RELAY_SLOTS = 2
 LATE = 2
-PIECES = 4
+PIECES = 8
 
 
 def split(x):
@@ -243,7 +243,7 @@
     passed = 0
     if square:
         for q in range(Q):
-            until = min(RELAY_SLOTS * (q + 1), min(row[0] for row in early))
+            until = min(RELAY_SLOTS * (q + 1) - q // 2, min(row[0] for row in early))
             lax.fori_loop(passed, until, slot, 0)
             passed = until
             landed(cols.at[q, pl.ds(0, 2 * NC), :], crecv.at[q])

time: 39.8 us -> 39.9 us (level)
  no operation moved by 1% of the time
where the time goes in v8:
time: 39.9 us; the launch traced here: 39.7 us
  Pallas kernels  39.1 us (98%)
  between operations  0.64 us (2%)
    pallas_call x1, Pallas kernels, local(): pl.pallas_call(functools.partial(kernel, R, C), out_shape=tuple((pltpu.VM...  38.1 us
    pallas_call x1, Pallas kernels, local(): pl.pallas_call(put, out_shape=tuple((jax.ShapeDtypeStruct(s, f32) for s i...  0.96 us

profile of v8, /device:TPU:0, one launch (start us, length us, event | category | flops | bytes accessed | tf_op | source)
XLA Modules:
  0.0 39.7 jit_solution(7823616388954442300)
XLA Ops:
  0.6 38.1 %shard_map.76 = (f32[512,256]{1,0:T(8,128)S(1)}, f32[64,512]{1,0:T(8,128)S(1)}, f32[64,512]{1,0:T(8,128)S(1)}) custom-call(f32[64,512]{1,0:T(8,128)} %fr.1, f32[64,512]{1,0:T(8,128)} %fc.1, f32[64,1024]{1,0:T(8,128)} %pr.1, f32[64,1024]{1,0:T(8,128)} %pc.1, f32[512,256]{1,0:T(8,128)} %acc.1), custom_call_target="tpu_custom_call" | custom-call | tf_op jit(solution)/shard_map/pallas_call | solution.py:541
  38.8 1.0 %shard_map.77 = (f32[512,256]{1,0:T(8,128)}, f32[64,512]{1,0:T(8,128)}, f32[64,512]{1,0:T(8,128)}) custom-call(f32[512,256]{1,0:T(8,128)S(1)} %get-tuple-element.6.a, f32[64,512]{1,0:T(8,128)S(1)} %get-tuple-element.7.b, f32[64,512]{1,0:T(8,128)S(1)} %get-tuple-element.8.c), custom_call_target="tpu_custom_call" | custom-call | tf_op jit(solution)/shard_map/pallas_call | solution.py:560

commit v9 on v8

--- a/solution.py
+++ b/solution.py
@@ -385,7 +385,6 @@
     stops = [by_place(need, pairs - 1)] + [by_place([[row[-1] - 2 + i] for row in need], 0) for i in range(3)]
     stops = [jnp.maximum(stops[0], stop) for stop in stops]
     f, w = weigh(final)
-    row_part(final, f, w)
     col_part(f, w)
 
     def push_grad(p, carry):
@@ -409,6 +408,7 @@
             grad_across(axis).start()
     else:
         lax.fori_loop(1, R, push_grad, 0)
+    row_part(final, f, w)
     upto(stops[0], stops[1])
     if square:
         for axis in range(2):

time: 39.9 us -> 40.2 us (level)
  no operation moved by 1% of the time
where the time goes in v9:
time: 40.2 us; the launch traced here: 40 us
  Pallas kernels  39.4 us (98%)
  between operations  0.64 us (2%)
    pallas_call x1, Pallas kernels, local(): pl.pallas_call(functools.partial(kernel, R, C), out_shape=tuple((pltpu.VM...  38.4 us
    pallas_call x1, Pallas kernels, local(): pl.pallas_call(put, out_shape=tuple((jax.ShapeDtypeStruct(s, f32) for s i...  0.96 us

profile of v9, /device:TPU:0, one launch (start us, length us, event | category | flops | bytes accessed | tf_op | source)
XLA Modules:
  0.0 40.0 jit_solution(1607449617945645142)
XLA Ops:
  0.6 38.4 %shard_map.76 = (f32[512,256]{1,0:T(8,128)S(1)}, f32[64,512]{1,0:T(8,128)S(1)}, f32[64,512]{1,0:T(8,128)S(1)}) custom-call(f32[64,512]{1,0:T(8,128)} %fr.1, f32[64,512]{1,0:T(8,128)} %fc.1, f32[64,1024]{1,0:T(8,128)} %pr.1, f32[64,1024]{1,0:T(8,128)} %pc.1, f32[512,256]{1,0:T(8,128)} %acc.1), custom_call_target="tpu_custom_call" | custom-call | tf_op jit(solution)/shard_map/pallas_call | solution.py:541
  39.1 1.0 %shard_map.77 = (f32[512,256]{1,0:T(8,128)}, f32[64,512]{1,0:T(8,128)}, f32[64,512]{1,0:T(8,128)}) custom-call(f32[512,256]{1,0:T(8,128)S(1)} %get-tuple-element.6.a, f32[64,512]{1,0:T(8,128)S(1)} %get-tuple-element.7.b, f32[64,512]{1,0:T(8,128)S(1)} %get-tuple-element.8.c), custom_call_target="tpu_custom_call" | custom-call | tf_op jit(solution)/shard_map/pallas_call | solution.py:560
